TPU v7x, 256 devices: a whole 4x4x8 slice. The times are simulated.
256 devices in a mesh: seq: 64 (over z, y, core), tp: 4 (over x).
Axes of the slice: x: 4, y: 4, z: 8, core: 2. Of those that a mesh axis runs over, the one named last changes fastest.
Arguments:
- tokens: bfloat16 [128, 1536], replicated, may hold values from -6 to 6
- attn_gain: float32 [1536], replicated, may hold values from 0.25 to 1.75
- qkv_weight: bfloat16 [1536, 2560], P(None, 'tp'), may hold values from -0.15625 to 0.15625
- out_weight: bfloat16 [1536, 1536], P(None, 'tp'), may hold values from -0.15625 to 0.15625
- moe_gain: float32 [1536], P('tp'), may hold values from 0.25 to 1.75
- router_weight: bfloat16 [1536, 40], P('tp'), may hold values from -0.3125 to 0.3125
- expert_gate: bfloat16 [40, 1536, 512], P(None, 'tp', 'seq'), may hold values from -0.15625 to 0.15625
- expert_up: bfloat16 [40, 1536, 512], P(None, 'tp', 'seq'), may hold values from -0.15625 to 0.15625
- expert_down: bfloat16 [40, 512, 1536], P(None, 'seq', 'tp'), may hold values from -0.375 to 0.375
- cache_keys: bfloat16 [32, 2048, 512], P(None, 'seq', 'tp'), may hold values from -240 to 240, as said below
- cache_values: bfloat16 [32, 2048, 512], P(None, 'seq', 'tp'), may hold values from -8 to 8
- lengths: int32 [32], replicated, may hold values from 1 to 32768, as said below
- routes: int32 [128, 8], replicated, may hold values from 0 to 39, all different within a row
Outputs:
- layer_out: bfloat16 [128, 1536], P(None, 'tp')
Inputs may be any that keep to these rules, and one draw needn't show every extreme that they name: `lengths`: one request has exactly 32768 cached positions. `cache_keys`: cached keys are already rotated.
All inputs are finite; a program needn't handle non-finite values.
Results may differ from a plain program's by a relative error of at most 0.014.
Values may be sent and summed in bfloat16 or wider, within the bound.
No kernel may reach another device: no remote copies, remote signals or barrier semaphores. Data moves between devices by JAX's collectives and lax.ppermute only.
A program may use at most 128 MiB of HBM per device.

v0:
```python
import jax
import jax.numpy as jnp
from jax import lax
from jax.sharding import PartitionSpec as P

D = 1536
HEAD = 64
EXPERTS = 40
SINK = 4
NEW = 4
GROUP = 3


EPSILON = 1e-06
ROPE_BASE = 10000.0
FLOOR_SCORE = -1e30


def joined(shard, axis, combine):
    everything = jax.tree.map(lambda part: lax.all_gather(part, axis), shard)
    initial = jax.tree.map(lambda part: part[0], everything)

    def lap(k, so_far):
        return combine(so_far, jax.tree.map(lambda part: part[k], everything))

    return lax.fori_loop(1, lax.axis_size(axis), lap, initial)


def rms_scale(values, gain):
    return values * lax.rsqrt(jnp.mean(values * values, axis=-1, keepdims=True) + EPSILON) * gain


def rotate(values, places):
    half_dim = values.shape[-1] // 2
    freqs = jnp.exp(-jnp.log(ROPE_BASE) * jnp.arange(half_dim, dtype=jnp.float32) / half_dim)
    angles = places.reshape((-1,) + (1,) * (values.ndim - 1)) * freqs
    cosine = jnp.cos(angles)
    sine = jnp.sin(angles)
    first = values[..., :half_dim]
    second = values[..., half_dim:]
    return jnp.concatenate(
        [first * cosine - second * sine, first * sine + second * cosine], axis=-1
    )


def visible(slots, lengths, window):
    lens = lengths[:, None]
    slot_row = slots[None, :]
    live = slot_row < lens
    older = lens - 1 - jnp.mod(lens - 1 - slot_row, window)
    placed = jnp.where(slot_row < SINK, slot_row, older)
    offsets = jnp.arange(NEW, dtype=jnp.int32)
    inside = (slot_row[:, None, :] < SINK) | (
        placed[:, None, :] >= lens[:, :, None] + offsets[None, :, None] - window
    )
    return live[:, None, :] & inside


def combine_parts(earlier, later):
    top_a, mass_a, weighted_a = earlier
    top_b, mass_b, weighted_b = later
    top_both = jnp.maximum(top_a, top_b)
    factor_a = jnp.exp(top_a - top_both)
    factor_b = jnp.exp(top_b - top_both)
    return (
        top_both,
        mass_a * factor_a + mass_b * factor_b,
        weighted_a * factor_a[..., None] + weighted_b * factor_b[..., None],
    )


def on_device(
    tokens,
    attn_gain,
    qkv_weight,
    out_weight,
    moe_gain,
    router_weight,
    expert_gate,
    expert_up,
    expert_down,
    cache_keys,
    cache_values,
    lengths,
    routes,
):
    seq_count = lax.axis_size("seq")
    seq_index = lax.axis_index("seq")
    tp_index = lax.axis_index("tp")
    token_count = tokens.shape[0]
    requests = cache_keys.shape[0]
    slot_count = cache_keys.shape[1]
    window = slot_count * seq_count - SINK
    local_kv = cache_keys.shape[2] // HEAD
    token_full = tokens.astype(jnp.float32)
    normed = rms_scale(token_full, attn_gain).astype(jnp.bfloat16)
    projected = jnp.dot(normed, qkv_weight, preferred_element_type=jnp.float32)
    projected = projected.reshape(token_count, local_kv, GROUP + 2, HEAD)
    places = (
        (lengths[:, None] + jnp.arange(NEW, dtype=jnp.int32)[None, :])
        .reshape(token_count)
        .astype(jnp.float32)
    )
    queries = rotate(projected[:, :, :GROUP], places).astype(jnp.bfloat16)
    new_keys = rotate(projected[:, :, GROUP], places).astype(jnp.bfloat16)
    new_values = projected[:, :, GROUP + 1].astype(jnp.bfloat16)
    query_b = queries.reshape(requests, NEW, local_kv, GROUP, HEAD)
    key_new = new_keys.reshape(requests, NEW, local_kv, HEAD)
    value_new = new_values.reshape(requests, NEW, local_kv, HEAD)
    slots = seq_index * slot_count + jnp.arange(slot_count, dtype=jnp.int32)
    seen = visible(slots, lengths, window)[:, :, None, None, :]
    factor = 1.0 / HEAD**0.5
    key_old = cache_keys.reshape(requests, slot_count, local_kv, HEAD)
    value_old = cache_values.reshape(requests, slot_count, local_kv, HEAD)
    old_scores = (
        jnp.einsum("rtgqd,rsgd->rtgqs", query_b, key_old, preferred_element_type=jnp.float32)
        * factor
    )
    new_scores = (
        jnp.einsum("rtgqd,rugd->rtgqu", query_b, key_new, preferred_element_type=jnp.float32)
        * factor
    )
    causal = jnp.arange(NEW)[:, None] >= jnp.arange(NEW)[None, :]
    own_mask = causal[None, :, None, None, :] & (seq_index == 0)
    old_masked = jnp.where(seen, old_scores, FLOOR_SCORE)
    new_masked = jnp.where(own_mask, new_scores, FLOOR_SCORE)
    top_score = jnp.maximum(jnp.max(old_masked, axis=-1), jnp.max(new_masked, axis=-1))
    old_weights = jnp.where(seen, jnp.exp(old_masked - top_score[..., None]), 0.0)
    new_weights = jnp.where(own_mask, jnp.exp(new_masked - top_score[..., None]), 0.0)
    mass = jnp.sum(old_weights, axis=-1) + jnp.sum(new_weights, axis=-1)
    weighted = jnp.einsum(
        "rtgqs,rsgd->rtgqd", old_weights, value_old.astype(jnp.float32)
    ) + jnp.einsum("rtgqu,rugd->rtgqd", new_weights, value_new.astype(jnp.float32))
    top_score, mass, weighted = joined((top_score, mass, weighted), "seq", combine_parts)
    attended = (weighted / mass[..., None]).reshape(token_count, -1).astype(jnp.bfloat16)
    feature_part = out_weight.shape[1]
    attn_out = jnp.dot(
        lax.all_gather(attended, "tp", axis=1, tiled=True),
        out_weight,
        preferred_element_type=jnp.float32,
    )
    residual = (
        lax.dynamic_slice_in_dim(token_full, tp_index * feature_part, feature_part, 1) + attn_out
    )
    gained = residual * moe_gain
    squares_local = jnp.sum(residual * residual, axis=-1)
    router_f = router_weight.astype(jnp.float32)
    squares_total = lax.psum(squares_local, "tp")
    scale = lax.rsqrt(squares_total / D + EPSILON)
    logits = lax.psum(
        jnp.dot(gained * scale[:, None], router_f, precision=lax.Precision.HIGHEST), "tp"
    )
    moe_in = (gained * scale[:, None]).astype(jnp.bfloat16)
    chosen = jnp.take_along_axis(logits, routes, axis=1)
    gate_prob = jax.nn.softmax(chosen, axis=-1)
    gate_part = jnp.einsum("td,edf->tef", moe_in, expert_gate, preferred_element_type=jnp.float32)
    up_part = jnp.einsum("td,edf->tef", moe_in, expert_up, preferred_element_type=jnp.float32)
    gate_pick = jnp.take_along_axis(gate_part, routes[:, :, None], axis=1)
    up_pick = jnp.take_along_axis(up_part, routes[:, :, None], axis=1)
    gate_sum, up_sum = (
        lax.psum(gate_pick.astype(jnp.bfloat16), "tp").astype(jnp.float32),
        lax.psum(up_pick.astype(jnp.bfloat16), "tp").astype(jnp.float32),
    )
    activated = (jax.nn.silu(gate_sum) * up_sum).astype(jnp.bfloat16)
    scaled = (gate_prob[:, :, None] * activated.astype(jnp.float32)).astype(jnp.bfloat16)
    onehot = (routes[:, :, None] == jnp.arange(EXPERTS, dtype=jnp.int32)[None, None, :]).astype(
        jnp.bfloat16
    )
    spread = jnp.einsum("tke,tkf->tef", onehot, scaled, preferred_element_type=jnp.float32).astype(
        jnp.bfloat16
    )
    moe_part = jnp.einsum("tef,efd->td", spread, expert_down, preferred_element_type=jnp.float32)
    moe_out = lax.psum(moe_part, "seq")
    return (residual + moe_out).astype(jnp.bfloat16)


def solution(mesh):
    in_specs = (
        P(),
        P(),
        P(None, "tp"),
        P(None, "tp"),
        P("tp"),
        P("tp", None),
        P(None, "tp", "seq"),
        P(None, "tp", "seq"),
        P(None, "seq", "tp"),
        P(None, "seq", "tp"),
        P(None, "seq", "tp"),
        P(),
        P(),
    )
    out_specs = P(None, "tp")
    return jax.shard_map(
        on_device, mesh=mesh, in_specs=in_specs, out_specs=out_specs, check_vma=False
    )
```

profile of v0, /device:TPU:1, one launch (start us, length us, event | category | flops | bytes accessed | tf_op | source)
XLA Modules:
  0.0 647.9 jit_solution(3661215171053748610)
XLA Ops:
  9.3 2.0 fusion.11
  13.8 1.2 reshape.397
  16.1 1.5 fusion.59
  21.6 62.0 %all-gather.1 = f32[2048,4,2,3]{1,2,3,0:T(2,128)S(1)} all-gather(f32[32,4,2,3]{1,2,3,0:T(2,128)S(1)} %copy.167), channel_id=3, replica_groups=mesh['seq'=64,'tp'=4] {'seq'}, dimensions={0}, use_global_device_ids=true | all-gather | bytes 199680 | tf_op jit(solution)/shard_map/all_gather | solution.py:20
  83.6 2.7 copy-done.1
  86.3 8.5 %copy.178 = f32[64,32,4,2,3]{1,3,4,2,0:T(2,128)} copy(f32[64,32,4,2,3]{2,3,4,1,0:T(2,128)} %bitcast.82) | data formatting | bytes 393216 | tf_op jit(solution)/shard_map/while | solution.py:26
  94.9 61.2 %all-gather = f32[2048,4,2,3]{1,2,3,0:T(2,128)S(1)} all-gather(f32[32,4,2,3]{1,2,3,0:T(2,128)S(1)} %copy.166), channel_id=2, replica_groups=mesh['seq'=64,'tp'=4] {'seq'}, dimensions={0}, use_global_device_ids=true | all-gather | bytes 199680 | tf_op jit(solution)/shard_map/all_gather | solution.py:20
  156.2 2.7 copy-done.2
  158.9 8.7 %copy.177 = f32[64,32,4,2,3]{1,3,4,2,0:T(2,128)} copy(f32[64,32,4,2,3]{2,3,4,1,0:T(2,128)} %bitcast.83) | data formatting | bytes 393216 | tf_op jit(solution)/shard_map/while | solution.py:26
  170.0 199.7 %while.19 = (s32[]{:T(128)}, f32[32,4,2,3]{0,2,3,1:T(2,128)S(1)}, f32[32,4,2,3]{0,2,3,1:T(2,128)S(1)}, f32[32,4,2,3,64]{4,3,2,1,0:T(4,128)S(1)}, f32[64,32,4,2,3...) while((s32[]{:T(128)}, f32[32,4,2,3]{0,2,3,1:T(2,128)S(1)}, ...), condition=%wide.region_6.7_spmd, body=%wide.region_5.6_spmd.sunk | while | flops 152069 | bytes 1026199 | solution.py:26
  370.5 10.6 %all_gather.21 = bf16[128,1536]{1,0:T(8,128)(2,1)S(1)} all-gather(bf16[128,384]{1,0:T(8,128)(2,1)S(1)} %convert_element_type.75), channel_id=1, replica_groups=mesh['seq'=64,'tp'=4] {'tp'}, dimensions={1}, use_global_device_ids=true | all-gather | bytes 491520 | tf_op jit(solution)/shard_map/all_gather | solution.py:138
  381.1 1.7 multiply_reduce_fusion.1
  382.8 7.4 %psum.35 = f32[128]{0:T(128)S(1)} all-reduce(f32[128]{0:T(128)S(1)} %get-tuple-element.256), channel_id=1, replica_groups=mesh['seq'=64,'tp'=4] {'tp'}, use_global_device_ids=true, to_apply=%region_8.9 | all-reduce | flops 128 | bytes 1024 | tf_op jit(solution)/shard_map/psum | solution.py:148
  391.7 1.8 copy.191
  393.5 10.5 %gather_fusion.2 = bf16[1024,8]{1,0:T(8,128)(2,1)} fusion(bf16[128,40,8]{2,1,0:T(8,128)(2,1)S(1)} %copy.191, s32[1024]{0:T(1024)S(1)} %reshape.431), kind=kCustom, calls=%fused_computation.1.clone | custom fusion | bytes 40960 | tf_op jit(solution)/shard_map/jit(take_along_axis)/gather | solution.py:159
  404.0 1.7 copy.193
  405.7 1.9 fusion.20
  407.6 1.8 copy.186
  409.4 10.5 %gather_fusion.1 = bf16[1024,8]{1,0:T(8,128)(2,1)} fusion(bf16[128,40,8]{2,1,0:T(8,128)(2,1)S(1)} %copy.186, s32[1024]{0:T(1024)S(1)} %reshape.431), kind=kCustom, calls=%fused_computation.clone | custom fusion | bytes 40960 | tf_op jit(solution)/shard_map/jit(take_along_axis)/gather | solution.py:158
  422.1 10.9 %psum.36 = f32[128,40]{0,1:T(8,128)S(1)} all-reduce(f32[128,40]{0,1:T(8,128)S(1)} %fusion.29), channel_id=1, replica_groups=mesh['seq'=64,'tp'=4] {'tp'}, use_global_device_ids=true, to_apply=%region_9.10 | all-reduce | flops 5120 | bytes 40960 | tf_op jit(solution)/shard_map/psum | solution.py:150
  433.1 7.0 %gather_fusion = f32[1024]{0:T(1024)S(1)} fusion(f32[128,40]{0,1:T(8,128)S(1)} %psum.36, s32[1024]{0:T(1024)S(1)} %reshape.411), kind=kCustom, calls=%fused_computation.2 | custom fusion | bytes 16384 | tf_op jit(solution)/shard_map/jit(take_along_axis)/gather | solution.py:154
  440.4 12.1 %all-reduce = (bf16[128,8,8]{0,2,1:T(8,128)(2,1)S(1)}, bf16[128,8,8]{0,2,1:T(8,128)(2,1)S(1)}) all-reduce(bf16[128,8,8]{0,2,1:T(8,128)(2,1)S(1)} %get-tuple-element.247, bf16[128,8,8]{0,2,1:T(8,128)(2,1)S(1)} %get-tuple-element.246), channel_id=1, replica_groups=mesh['seq'=64,'tp'=4] {'tp'}, use_global_device_ids=true, to_apply=%region_13.15 | all-reduce | flops 16384 | bytes 65536 | tf_op jit(solution)/shard_map/psum | solution.py:162
  454.3 185.2 %all-reduce.3.cloned.1.call-done = f32[128,384]{1,0:T(8,128)} async-done(((f32[128,384]{1,0:T(8,128)}), f32[128,384]{1,0:T(8,128)}) %all-reduce.3.cloned.1.call-update) | async-done | bytes 196624 | tf_op jit(solution)/shard_map/psum | solution.py:173
  639.5 1.6 add_convert_fusion
  (416 shorter events, 216.3 us)
Async XLA Ops:
  6.5 2.7 copy-start
  6.5 4.7 copy-start.15
  6.5 162.3 %all-gather.5.cloned.1.call-start = ((), (), s32[]{:S(2)}) async-start(), calls=%async_computation.1 | async-start | bytes 25559040 | tf_op jit(solution)/shard_map/all_gather | solution.py:20
  9.3 2.8 copy-start.6
  15.1 1.0 copy-start.10
  15.1 1.0 copy-start.11
  16.1 2.0 copy-start.4
  18.1 1.3 copy-start.3
  18.1 2.7 copy-start.5
  19.4 620.1 %all-reduce.3.cloned.1.call-start = ((), (), s32[]{:S(2)}) async-start(), calls=%async_computation | async-start | bytes 393216 | tf_op jit(solution)/shard_map/psum | solution.py:173
  83.6 2.7 copy-start.1
  156.2 2.7 copy-start.2
  158.9 8.9 %copy-start.9 = (s32[128,8]{0,1:T(8,128)S(1)}, s32[128,8]{0,1:T(8,128)}, u32[]{:S(2)}) copy-start(s32[128,8]{0,1:T(8,128)} %param.29) | copy-start | bytes 12292
  369.7 21.0 %copy-start.7 = (bf16[40,384,8]{1,2,0:T(8,128)(2,1)S(1)}, bf16[40,384,8]{1,2,0:T(8,128)(2,1)}, u32[]{:S(2)}) copy-start(bf16[40,384,8]{1,2,0:T(8,128)(2,1)} %param.24) | copy-start | bytes 737284
  369.7 21.0 %copy-start.13 = (f32[384]{0:T(512)S(1)}, f32[384]{0:T(512)}, u32[]{:S(2)}) copy-start(f32[384]{0:T(512)} %param.21) | copy-start | bytes 4612
  390.3 0.5 copy-start.14
  433.1 7.3 %copy-start.12 = (bf16[128,8,8]{0,2,1:T(8,128)(2,1)S(1)}, bf16[128,8,8]{0,2,1:T(8,128)(2,1)}, u32[]{:S(2)}) copy-start(bf16[128,8,8]{0,2,1:T(8,128)(2,1)} %copy.193) | copy-start | bytes 49156
  433.1 7.3 %copy-start.16 = (pred[128,8]{0,1:T(8,128)(4,1)S(1)}, pred[128,8]{0,1:T(8,128)(4,1)}, u32[]{:S(2)}) copy-start(pred[128,8]{0,1:T(8,128)(4,1)} %and_bitcast_fusion) | copy-start | bytes 3076
  440.1 13.2 %copy-start.8 = (bf16[40,8,384]{2,1,0:T(8,128)(2,1)S(1)}, bf16[40,8,384]{2,1,0:T(8,128)(2,1)}, u32[]{:S(2)}) copy-start(bf16[40,8,384]{2,1,0:T(8,128)(2,1)} %param.25) | copy-start | bytes 737284
Sparse Core Ops, SparseCore 0:
  19.5 145.9 all-gather.4
  454.4 185.0 all-reduce.2
where the time goes:
time: 659 us; the launch traced here: 648 us
  waiting for transfers between devices  185 us (28%)
  blocking collectives  164 us (25%)
  local copies, waits for them, and re-layouts  150 us (23%)
  other arithmetic  119 us (18%)
  between operations  13.9 us (2%)
  matrix products  12.6 us (2%)
    psum x1, waiting for transfers between devices, on_device(): moe_out = lax.psum(moe_part, 'seq')  185 us
    all_gather x2, blocking collectives, joined(): everything = jax.tree.map(lambda part: lax.all_gather(part, axis), shard)  123 us
    dynamic_slice x63, local copies, waits for them, and re-layouts, lap(): return combine(so_far, jax.tree.map(lambda part: part[k], everything))  65.7 us
    add x63, other arithmetic, combine_parts(): weighted_a * factor_a[..., None] + weighted_b * factor_b[..., None]  62.8 us
    add x63, other arithmetic, combine_parts(): mass_a * factor_a + mass_b * factor_b  48.3 us
    while x6, local copies, waits for them, and re-layouts, joined(): return lax.fori_loop(1, lax.axis_size(axis), lap, initial)  17.7 us
  transfers between devices with their start and end apart: 2, of which 1 were waited for; matrix products, arithmetic and copies ran while one was open for 3% of the time, Pallas kernels for 0%

commit v1 on v0

v1 whole, which is shorter than its diff:
```python
import functools

import jax
import jax.numpy as jnp
from jax import lax
from jax.experimental import pallas as pl
from jax.experimental.pallas import tpu as pltpu
from jax.sharding import Mesh, PartitionSpec as P

D = 1536
HEAD = 64
EXPERTS = 40
TOP = 8
SINK = 4
NEW = 4
GROUP = 3
REQS = 32
TOKENS = 128
WINDOW = 2044
SLOTS = 32
FEAT = 384
FF = 8

EPSILON = 1e-06
ROPE_BASE = 10000.0
FLOOR_SCORE = -1e30

F32 = jnp.float32
BF16 = jnp.bfloat16
VMEM = pl.BlockSpec(memory_space=pltpu.VMEM)
SMEM = pl.BlockSpec(memory_space=pltpu.SMEM)


def iota(shape, dim):
    return lax.broadcasted_iota(jnp.int32, shape, dim)


def dot(a, b):
    return jnp.dot(a, b, preferred_element_type=F32)


def dot_t(a, b):
    return lax.dot_general(a, b, (((1,), (1,)), ((), ())), preferred_element_type=F32)


def call(body, outs, n_in, smem=(), scratch=(), flops=10**7):
    return pl.pallas_call(
        body,
        out_shape=outs,
        in_specs=[SMEM if i in smem else VMEM for i in range(n_in)],
        out_specs=jax.tree.map(lambda _: VMEM, outs),
        scratch_shapes=list(scratch),
        cost_estimate=pl.CostEstimate(flops=flops, bytes_accessed=10**6, transcendentals=0),
    )


def attend_body(len_ref, tok_ref, gain_ref, w_ref, cos_ref, sin_ref, k_ref, v_ref, keep_ref, send_ref):
    core = lax.axis_index("core")
    seq = (lax.axis_index("z") * 4 + lax.axis_index("y")) * 2 + core
    x = tok_ref[...].astype(F32)
    normed = x * lax.rsqrt(jnp.mean(x * x, axis=-1, keepdims=True) + EPSILON) * gain_ref[...]
    proj = dot(normed.astype(BF16), w_ref[...])
    cos = cos_ref[...]
    sin = sin_ref[...]
    lane = iota((TOKENS, 128), 1)
    low = lane < 64
    first = (lane % 64) < 32
    tiles = [proj[:, 128 * i : 128 * i + 128] for i in range(5)]

    def rot(t):
        swapped = jnp.where(first, pltpu.roll(t, 96, 1), pltpu.roll(t, 32, 1))
        return t * cos + swapped * sin

    turned = [rot(t) for t in tiles]
    query = []
    for g in range(2):
        for q in range(GROUP):
            at = g * 5 + q
            t = turned[at // 2]
            if at % 2 != g:
                t = pltpu.roll(t, 64, 1)
            query.append(jnp.where(low if g == 0 else ~low, t * 0.125, 0.0).astype(BF16))
    key_new = jnp.where(low, pltpu.roll(turned[1], 64, 1), pltpu.roll(turned[4], 64, 1)).astype(BF16)
    value_new = jnp.where(low, tiles[2], tiles[4]).astype(BF16)

    row = iota((32, 256), 0)
    col = iota((32, 256), 1)
    same = (row // NEW) == (col // SLOTS)
    slot = seq * SLOTS + col % SLOTS
    nrow = iota((32, 32), 0)
    ncol = iota((32, 32), 1)
    ok_new = (nrow // NEW == ncol // NEW) & (ncol <= nrow) & (seq == 0)
    glow = iota((32, 128), 1) < 64
    glane = iota((32, 128), 1)
    for grp in range(4):
        lens = jnp.zeros((32, 256), jnp.int32)
        for r in range(8):
            lens = jnp.where(row // NEW == r, len_ref[grp * 8 + r], lens)
        back = lens - 1 - slot
        live = back >= 0
        safe = jnp.maximum(back, 0)
        age = safe - ((safe * 32833) >> 26) * WINDOW
        ok = same & live & ((slot < SINK) | (age <= WINDOW - 1 - row % NEW))
        rows = slice(grp * 32, grp * 32 + 32)
        qg = jnp.concatenate([b[rows] for b in query], axis=0)
        s = dot_t(qg, k_ref[grp * 256 : grp * 256 + 256, :]).reshape(6, 32, 256)
        sn = dot_t(qg, key_new[rows]).reshape(6, 32, 32)
        s = jnp.where(ok[None], s, FLOOR_SCORE)
        sn = jnp.where(ok_new[None], sn, FLOOR_SCORE)
        m = jnp.maximum(jnp.max(s, axis=-1, keepdims=True), jnp.max(sn, axis=-1, keepdims=True))
        p = jnp.where(ok[None], jnp.exp(s - m), 0.0)
        pn = jnp.where(ok_new[None], jnp.exp(sn - m), 0.0)
        mass = jnp.sum(p, axis=-1, keepdims=True) + jnp.sum(pn, axis=-1, keepdims=True)
        acc = dot(p.reshape(192, 256).astype(BF16), v_ref[grp * 256 : grp * 256 + 256, :]) + dot(
            pn.reshape(192, 32).astype(BF16), value_new[rows]
        )
        some = mass > 0.0
        mass = jnp.where(some, mass, 1.0)
        acc = acc.reshape(6, 32, 128) / mass
        lse = jnp.where(some, m + jnp.log(mass), FLOOR_SCORE)
        packed = []
        for g in range(2):
            a = [acc[g * 3 + q] for q in range(3)]
            a = [b if q % 2 == g else pltpu.roll(b, 64, 1) for q, b in enumerate(a)]
            e = [lse[g * 3 + q] for q in range(3)]
            stats = jnp.where(glane == 64, e[0], jnp.where(glane == 65, e[1], jnp.where(glane == 66, e[2], 0.0)))
            packed.append((jnp.where(glow, a[0], a[1]), jnp.where(glow, a[2], stats)))
        mine = core == 0
        for i in range(2):
            lanes = slice(128 * i, 128 * i + 128)
            keep_ref[rows, lanes] = jnp.where(mine, packed[0][i], packed[1][i])
            send_ref[rows, lanes] = jnp.where(mine, packed[1][i], packed[0][i])


def merge(parts):
    top = functools.reduce(jnp.maximum, [e for _, _, e in parts])
    weights = [jnp.exp(e - top) for _, _, e in parts]
    total = sum(weights)
    lo = hi = 0.0
    glow = iota(total.shape, 1) < 64
    for w, (a, b, _) in zip(weights, parts):
        w = w / total
        lo = lo + a * jnp.where(glow, w[:, 64:65], w[:, 65:66])
        hi = hi + b * w[:, 66:67]
    return lo, hi, top + jnp.log(total)


def encode(lo, hi, lse):
    lane = iota(lse.shape, 1)
    a = lse.astype(BF16).astype(F32)
    b = (lse - a).astype(BF16).astype(F32)
    c = lse - a - b
    tail = jnp.where(lane < 67, a, jnp.where(lane < 70, pltpu.roll(b, 3, 1), pltpu.roll(c, 6, 1)))
    tail = jnp.where(lane < 73, tail, 0.0)
    return lo.astype(BF16), jnp.where(lane < 64, hi, tail).astype(BF16)


def decode(block):
    lo = block[:, :128].astype(F32)
    hi = block[:, 128:].astype(F32)
    lse = hi + pltpu.roll(hi, 125, 1) + pltpu.roll(hi, 122, 1)
    lane = iota(lse.shape, 1)
    return lo, hi, jnp.where((lane >= 64) & (lane < 67), lse, 0.0)


def merge_core_body(keep_ref, got_ref, out_ref):
    lane = iota((TOKENS, 128), 1)
    parts = []
    for ref in (keep_ref, got_ref):
        hi = ref[:, 128:]
        parts.append((ref[:, :128], hi, jnp.where(lane >= 64, hi, 0.0)))
    lo, hi = encode(*merge(parts))
    out_ref[:, :128] = lo
    out_ref[:, 128:] = hi


def merge_y_body(in_ref, out_ref):
    lo, hi = encode(*merge([decode(in_ref[i]) for i in range(4)]))
    for i in range(8):
        out_ref[i, :, :128] = lo
        out_ref[i, :, 128:] = hi


def merge_z_body(in_ref, out_ref):
    lo, hi, _ = merge([decode(in_ref[i]) for i in range(8)])
    lo = lo.astype(BF16)
    hi = hi.astype(BF16)
    for i in range(16):
        out_ref[i, :, :128] = lo
        out_ref[i, :, 128:] = hi


def split3(v):
    a = v.astype(BF16)
    r = v - a.astype(F32)
    b = r.astype(BF16)
    return a, b, (r - b.astype(F32)).astype(BF16)


def project_body(mine_ref, other_ref, tok_ref, w_ref, gain_ref, router_ref, gate_ref, up_ref, routes_ref, res_ref, out_ref):
    core = lax.axis_index("core")
    tp = lax.axis_index("tp")
    acc = tok_ref[:, pl.ds(pl.multiple_of(tp * FEAT, 128), FEAT)].astype(F32)
    for ref, c in ((mine_ref, core), (other_ref, 1 - core)):
        for x in range(4):
            a = jnp.concatenate([ref[y * 4 + x] for y in range(4)], axis=0)[:, :192]
            at = pl.multiple_of((2 * x + c) * 192, 64)
            acc = acc + dot(a, w_ref[pl.ds(at, 192), :])
    res_ref[...] = acc
    gained = acc * gain_ref[...]
    squares = jnp.sum(acc * acc, axis=-1, keepdims=True)
    router = router_ref[...]
    g0, g1, g2 = split3(gained)
    logits = dot_t(g0, router) + dot_t(g1, router) + dot_t(g2, router)
    both = jnp.concatenate([dot_t(g0, gate_ref[...]), dot_t(g0, up_ref[...])], axis=1)
    routes = routes_ref[...]
    expert = (iota((TOKENS, 640), 1) % 320) // FF
    elane = iota((TOKENS, EXPERTS), 1)
    lane = iota((TOKENS, 128), 1)
    frow = iota((640, 128), 0)
    fcol = iota((640, 128), 1)
    fold = (frow % FF == fcol % FF) & (frow // 320 == fcol // 64)
    picks = jnp.zeros((TOKENS, 128), F32)
    stats = jnp.where(lane == TOP, squares, 0.0)
    for k in range(TOP):
        r = routes[:, k : k + 1]
        chosen = jnp.sum(jnp.where(elane == r, logits, 0.0), axis=-1, keepdims=True)
        stats = jnp.where(lane == k, chosen, stats)
        f = (fold & ((fcol % 64) // FF == k)).astype(BF16)
        picks = picks + dot(jnp.where(expert == r, both, 0.0).astype(BF16), f)
    a, b, c = (v.astype(F32) for v in split3(stats))
    tail = (a + pltpu.roll(b, 16, 1) + pltpu.roll(c, 32, 1)).astype(BF16)
    picks = picks.astype(BF16)
    for i in range(4):
        out_ref[i, :, :128] = picks
        out_ref[i, :, 128:] = tail


def expert_body(in_ref, routes_ref, down_ref, keep_ref, send_ref, part_ref):
    core = lax.axis_index("core")
    lane = iota((TOKENS, 128), 1)
    picks = sum(in_ref[i, :, :128].astype(F32) for i in range(4))
    tail = sum(in_ref[i, :, 128:].astype(F32) for i in range(4))
    stats = tail + pltpu.roll(tail, 112, 1) + pltpu.roll(tail, 96, 1)
    scale = lax.rsqrt(stats[:, TOP : TOP + 1] / D + EPSILON)
    logits = jnp.where(lane < TOP, stats * scale, FLOOR_SCORE)
    weights = jnp.exp(logits - jnp.max(logits, axis=-1, keepdims=True))
    prob = weights / jnp.sum(weights, axis=-1, keepdims=True)
    gate = picks * scale
    up = pltpu.roll(gate, 64, 1)
    activated = (gate / (1.0 + jnp.exp(-gate)) * up).astype(BF16).astype(F32)
    wide = jnp.zeros((TOKENS, 128), F32)
    for k in range(TOP):
        wide = jnp.where(lane // FF == k, prob[:, k : k + 1], wide)
    scaled = jnp.where(lane < 64, wide * activated, 0.0).astype(BF16)
    erow = iota((128, 1024), 0)
    ecol = iota((128, 1024), 1)
    spread_to = ((erow % FF == ecol % FF) & (erow // FF == ecol // 128)).astype(BF16)
    tiled = dot(scaled, spread_to)
    routes = routes_ref[...]
    spread = []
    for i in range(3):
        s = jnp.zeros((TOKENS, 128), F32)
        for k in range(TOP):
            s = jnp.where(lane // FF + 16 * i == routes[:, k : k + 1], tiled[:, 128 * k : 128 * k + 128], s)
        spread.append(s)
    spread = jnp.concatenate(spread, axis=1)[:, :320].astype(BF16)
    part_ref[...] = dot(spread, down_ref[...])
    keep_ref[...] = part_ref[pl.ds(pl.multiple_of(core * 64, 64), 64), :]
    send_ref[...] = part_ref[pl.ds(pl.multiple_of((1 - core) * 64, 64), 64), :]


def swap(v):
    return lax.ppermute(v, "core", [(0, 1), (1, 0)])


def exchange(v, axes):
    return lax.all_to_all(v, axes, 0, 0, tiled=True)


def on_device(
    tokens,
    attn_gain,
    qkv_weight,
    out_weight,
    moe_gain,
    router_weight,
    expert_gate,
    expert_up,
    expert_down,
    cache_keys,
    cache_values,
    lengths,
    routes,
):
    core = lax.axis_index("core")
    sds = jax.ShapeDtypeStruct
    places = (lengths[:, None] + jnp.arange(NEW, dtype=jnp.int32)[None, :]).reshape(TOKENS).astype(F32)
    half = HEAD // 2
    freqs = jnp.exp(-jnp.log(ROPE_BASE) * jnp.arange(half, dtype=F32) / half)
    angles = places[:, None] * jnp.tile(freqs, 4)[None, :]
    cos = jnp.cos(angles)
    sin = jnp.where(jnp.arange(128)[None, :] % 64 < half, -jnp.sin(angles), jnp.sin(angles))

    keep, send = call(attend_body, (sds((TOKENS, 256), F32),) * 2, 8, smem=(0,))(
        lengths,
        tokens,
        attn_gain.reshape(1, D),
        qkv_weight,
        cos,
        sin,
        cache_keys.reshape(REQS * SLOTS, 128),
        cache_values.reshape(REQS * SLOTS, 128),
    )
    packed = call(merge_core_body, sds((TOKENS, 256), BF16), 2)(keep, swap(send))
    packed = exchange(packed.reshape(4, 32, 256), "y")
    packed = call(merge_y_body, sds((8, 32, 256), BF16), 1)(packed)
    packed = exchange(packed, "z")
    packed = call(merge_z_body, sds((16, 32, 256), BF16), 1)(packed)
    mine = exchange(packed, ("y", "tp"))
    other = swap(mine)

    residual, picked = call(project_body, (sds((TOKENS, FEAT), F32), sds((4, TOKENS, 256), BF16)), 9)(
        mine,
        other,
        tokens,
        out_weight,
        moe_gain.reshape(1, FEAT),
        router_weight.T,
        expert_gate.transpose(0, 2, 1).reshape(EXPERTS * FF, FEAT),
        expert_up.transpose(0, 2, 1).reshape(EXPERTS * FF, FEAT),
        routes,
    )
    picked = exchange(picked, "tp")
    keep, send = call(
        expert_body,
        (sds((TOKENS // 2, FEAT), F32),) * 2,
        3,
        scratch=[pltpu.VMEM((TOKENS, FEAT), F32)],
    )(picked, routes, expert_down.reshape(EXPERTS * FF, FEAT))

    part = (keep + swap(send)).astype(BF16)
    part = exchange(jnp.broadcast_to(part, (4,) + part.shape), "y")
    part = jnp.sum(part.astype(F32), axis=0).astype(BF16)
    part = exchange(jnp.broadcast_to(part, (8,) + part.shape), "z")
    own = lax.dynamic_slice_in_dim(residual, core * (TOKENS // 2), TOKENS // 2, 0)
    own = (own + jnp.sum(part.astype(F32), axis=0)).astype(BF16)
    theirs = swap(own)
    first = core == 0
    return jnp.concatenate([jnp.where(first, own, theirs), jnp.where(first, theirs, own)], axis=0)


def solution(mesh):
    seq = ("z", "y", "core")
    grid = Mesh(mesh.devices.reshape(8, 4, 2, 4), seq + ("tp",))
    in_specs = (
        P(),
        P(),
        P(None, "tp"),
        P(None, "tp"),
        P("tp"),
        P("tp", None),
        P(None, "tp", seq),
        P(None, "tp", seq),
        P(None, seq, "tp"),
        P(None, seq, "tp"),
        P(None, seq, "tp"),
        P(),
        P(),
    )
    out_specs = P(None, "tp")
    return jax.shard_map(on_device, mesh=grid, in_specs=in_specs, out_specs=out_specs, check_vma=False)
```

time: 659 us -> 112 us (0.17); the launches traced: 648 us -> 111 us
  waiting for transfers between devices: 185 us -> 15.9 us
  local copies, waits for them, and re-layouts: 150 us -> 4.93 us
  other arithmetic: 119 us -> 3.39 us
  blocking collectives: 164 us -> 54.2 us
  Pallas kernels: 0 us -> 17 us
  starting transfers between devices: 0.04 us -> 15.3 us
  between operations: 13.9 us -> 0.09 us
  matrix products: 12.6 us -> 0 us
    psum x1 -> x0, waiting for transfers between devices: 185 us -> none  [on_device(): moe_out = lax.psum(moe_part, 'seq')]
    all_gather x3 -> x0, blocking collectives: 134 us -> none  [the longest x2 123 us: joined(): everything = jax.tree.map(lambda part: lax.all_gather(part, axis), shard)]
    add x128 -> x0, other arithmetic: 112 us -> none  [the longest x63 62.8 us: combine_parts(): weighted_a * factor_a[..., None] + weighted_b * factor_b[..., None]]
    dynamic_slice x63 -> x0, local copies, waits for them, and re-layouts: 65.7 us -> none  [lap(): return combine(so_far, jax.tree.map(lambda part: part[k], everything))]
    all_to_all x0 -> x5, blocking collectives: none -> 54.2 us  [exchange(): return lax.all_to_all(v, axes, 0, 0, tiled=True)]
    gather x11 -> x0, local copies, waits for them, and re-layouts: 31.4 us -> none  [the longest x2 12.2 us: on_device(): up_pick = jnp.take_along_axis(up_part, routes[:, :, None], axis=1)]
    psum x3 -> x0, blocking collectives: 30.5 us -> none  [the longest x1 12.1 us: on_device(): lax.psum(up_pick.astype(jnp.bfloat16), 'tp').astype(jnp.float32)]
    exp x126 -> x0, local copies, waits for them, and re-layouts: 20.5 us -> none  [the longest x63 10.3 us: combine_parts(): factor_a = jnp.exp(top_a - top_both)]
  transfers between devices with their start and end apart: 2 -> 5, of which waited for: 1 -> 4; matrix products, arithmetic and copies ran while one was open for 3% -> 1% of each run, Pallas kernels for 0% -> 0%
where the time goes in v1:
time: 112 us; the launch traced here: 111 us
  blocking collectives  54.2 us (48%)
  Pallas kernels  17 us (15%)
  waiting for transfers between devices  15.9 us (14%)
  starting transfers between devices  15.3 us (14%)
  local copies, waits for them, and re-layouts  4.93 us (4%)
  other arithmetic  3.39 us (3%)
    all_to_all x5, blocking collectives, exchange(): return lax.all_to_all(v, axes, 0, 0, tiled=True)  54.2 us
    all_to_all x1, waiting for transfers between devices, exchange(): return lax.all_to_all(v, axes, 0, 0, tiled=True)  12.7 us
    ppermute x4, starting transfers between devices, swap(): return lax.ppermute(v, 'core', [(0, 1), (1, 0)])  11.9 us
    pallas_call x1, Pallas kernels, on_device(): call(attend_body, (sds((TOKENS, 256), F32),) * 2, 8, smem=(0,))  4.8 us
    pallas_call x1, Pallas kernels, on_device(): call(project_body, (sds((TOKENS, FEAT), F32), sds((4, TOKENS, 256), BF16)...  3.86 us
    all_to_all x1, starting transfers between devices, exchange(): return lax.all_to_all(v, axes, 0, 0, tiled=True)  3.45 us
    ppermute x4, waiting for transfers between devices, swap(): return lax.ppermute(v, 'core', [(0, 1), (1, 0)])  3.24 us
    pallas_call x1, Pallas kernels, on_device(): call(expert_body, (sds((TOKENS // 2, FEAT), F32),) * 2, 3, scratch=[pltpu...  2.81 us
  transfers between devices with their start and end apart: 5, of which 4 were waited for; matrix products, arithmetic and copies ran while one was open for 1% of the time, Pallas kernels for 0%

profile of v1, /device:TPU:1, one launch (start us, length us, event | category | flops | bytes accessed | tf_op | source)
XLA Modules:
  0.0 110.8 jit_solution(13167016035542705889)
XLA Ops:
  1.0 1.3 %reshape.63.gain_ref = f32[1,1536]{1,0:T(1,128)} reshape(f32[1536]{0:T(1024)} %param.14) | data formatting | bytes 12288 | tf_op jit(solution)/shard_map/reshape | solution.py:308
  2.2 1.0 negate_select_fusion
  3.2 4.8 %shard_map.127 = (f32[128,256]{1,0:T(8,128)}, f32[128,256]{1,0:T(8,128)}) custom-call(s32[32]{0:T(128)} %len_ref.1, bf16[128,1536]{1,0:T(8,128)(2,1)} %tok_ref.3, f32[1,1536]{1,0:T(1,128)} %reshape.63.gain_ref, bf16[1536,640]{1,0:T(8,128)(2,1)} %w_ref.2, f32[128,128]{1,0:T(8,128)} %get-tuple-element.20.cos_ref, f32[128,128]{1,0:T(8,128)} %get-tuple-element.19.sin_ref, ...), custom_call_target="tpu_custom_call" | custom-call | flops 10000000 | bytes 1000000 | tf_op jit(solution)/shard_map/pallas_call | solution.py:305
  8.0 3.2 %collective-permute-start = (f32[128,256]{1,0:T(8,128)}, f32[128,256]{1,0:T(8,128)S(1)}, u32[]{:S(2)}, u32[]{:S(2)}) collective-permute-start(f32[128,256]{1,0:T(8,128)} %get-tuple-element.12), channel_id=1, source_target_pairs={{0,4},{4,0},{1,5},{5,1},{2,6},{6,2},{3,7},{7,3},{8,12},{12,8},{9,1... | collective-permute-start | bytes 393224 | tf_op jit(solution)/shard_map/ppermute | solution.py:274
  11.3 1.2 %collective-permute-done.got_ref = f32[128,256]{1,0:T(8,128)S(1)} collective-permute-done((f32[128,256]{1,0:T(8,128)}, f32[128,256]{1,0:T(8,128)S(1)}, u32[]{:S(2)}, u32[]{:S(2)}) %collective-permute-start) | collective-permute-done | bytes 131104 | tf_op jit(solution)/shard_map/ppermute | solution.py:274
  13.1 1.8 %shard_map.128 = bf16[128,256]{1,0:T(8,128)(2,1)} custom-call(f32[128,256]{1,0:T(8,128)} %get-tuple-element.11.keep_ref, f32[128,256]{1,0:T(8,128)} %copy-done.2), custom_call_target="tpu_custom_call" | custom-call | flops 10000000 | bytes 1000000 | tf_op jit(solution)/shard_map/pallas_call | solution.py:315
  14.9 8.4 %all_to_all.30.in_ref = bf16[4,32,256]{2,1,0:T(8,128)(2,1)} all-to-all(bf16[4,32,256]{2,1,0:T(8,128)(2,1)} %bitcast.13), channel_id=1, replica_groups=mesh['z'=8,'y'=4,'core'=2,'tp'=4] {'y'}, dimensions={0} | all-to-all | bytes 131072 | tf_op jit(solution)/shard_map/all_to_all | solution.py:278
  23.4 1.7 %shard_map.129 = bf16[8,32,256]{2,1,0:T(8,128)(2,1)} custom-call(bf16[4,32,256]{2,1,0:T(8,128)(2,1)} %all_to_all.30.in_ref), custom_call_target="tpu_custom_call" | custom-call | flops 10000000 | bytes 1000000 | tf_op jit(solution)/shard_map/pallas_call | solution.py:317
  25.1 14.9 %all_to_all.31.in_ref = bf16[8,32,256]{2,1,0:T(8,128)(2,1)} all-to-all(bf16[8,32,256]{2,1,0:T(8,128)(2,1)} %shard_map.129), channel_id=1, replica_groups=mesh['z'=8,'y'=4,'core'=2,'tp'=4] {'z'}, dimensions={0} | all-to-all | bytes 262144 | tf_op jit(solution)/shard_map/all_to_all | solution.py:278
  40.0 2.0 %shard_map.130 = bf16[16,32,256]{2,1,0:T(8,128)(2,1)} custom-call(bf16[8,32,256]{2,1,0:T(8,128)(2,1)} %all_to_all.31.in_ref), custom_call_target="tpu_custom_call" | custom-call | flops 10000000 | bytes 1000000 | tf_op jit(solution)/shard_map/pallas_call | solution.py:319
  42.0 12.3 %all_to_all.32.mine_ref = bf16[16,32,256]{2,1,0:T(8,128)(2,1)S(1)} all-to-all(bf16[16,32,256]{2,1,0:T(8,128)(2,1)} %shard_map.130), channel_id=1, replica_groups=mesh['z'=8,'y'=4,'core'=2,'tp'=4] {'y','tp'}, dimensions={0} | all-to-all | bytes 524288 | tf_op jit(solution)/shard_map/all_to_all | solution.py:278
  54.3 4.5 %collective-permute-start.1 = (bf16[16,32,256]{2,1,0:T(8,128)(2,1)S(1)}, bf16[16,32,256]{2,1,0:T(8,128)(2,1)S(1)}, u32[]{:S(2)}, u32[]{:S(2)}) collective-permute-start(bf16[16,32,256]{2,1,0:T(8,128)(2,1)S(1)} %all_to_all.32.mine_ref), channel_id=1, source_target_pairs={{0,4},{4,0},{1,5},{5,1},{2,6},{6,2},{3,7},{7,3},{8,12},{12,8},{9,1... | collective-permute-start | bytes 786440 | tf_op jit(solution)/shard_map/ppermute | solution.py:274
  60.8 3.9 %shard_map.131 = (f32[128,384]{1,0:T(8,128)}, bf16[4,128,256]{2,1,0:T(8,128)(2,1)}) custom-call(bf16[16,32,256]{2,1,0:T(8,128)(2,1)} %copy-done, bf16[16,32,256]{2,1,0:T(8,128)(2,1)} %copy-done.1, bf16[128,1536]{1,0:T(8,128)(2,1)} %tok_ref.3, bf16[1536,384]{1,0:T(8,128)(2,1)} %w_ref.3, f32[1,384]{1,0:T(1,128)} %reshape.67.gain_ref, ...), custom_call_target="tpu_custom_call" | custom-call | flops 10000000 | bytes 1000000 | tf_op jit(solution)/shard_map/pallas_call | solution.py:323
  64.7 10.7 %all_to_all.33.in_ref = bf16[4,128,256]{2,1,0:T(8,128)(2,1)} all-to-all(bf16[4,128,256]{2,1,0:T(8,128)(2,1)} %get-tuple-element.14), channel_id=1, replica_groups=mesh['z'=8,'y'=4,'core'=2,'tp'=4] {'tp'}, dimensions={0} | all-to-all | bytes 524288 | tf_op jit(solution)/shard_map/all_to_all | solution.py:278
  75.4 2.8 %shard_map.132 = (f32[64,384]{1,0:T(8,128)}, f32[64,384]{1,0:T(8,128)}) custom-call(bf16[4,128,256]{2,1,0:T(8,128)(2,1)} %all_to_all.33.in_ref, s32[128,8]{1,0:T(8,128)} %copy.18.routes_ref, bf16[320,384]{1,0:T(8,128)(2,1)} %bitcast.16), custom_call_target="tpu_custom_call" | custom-call | flops 10000000 | bytes 1000000 | tf_op jit(solution)/shard_map/pallas_call | solution.py:335
  78.2 1.1 %collective-permute-start.2 = (f32[64,384]{1,0:T(8,128)}, f32[64,384]{1,0:T(8,128)S(1)}, u32[]{:S(2)}, u32[]{:S(2)}) collective-permute-start(f32[64,384]{1,0:T(8,128)} %get-tuple-element.16), channel_id=1, source_target_pairs={{0,4},{4,0},{1,5},{5,1},{2,6},{6,2},{3,7},{7,3},{8,12},{12,8},{9,1... | collective-permute-start | bytes 294920 | tf_op jit(solution)/shard_map/ppermute | solution.py:274
  79.3 1.2 %collective-permute-done.2 = f32[64,384]{1,0:T(8,128)S(1)} collective-permute-done((f32[64,384]{1,0:T(8,128)}, f32[64,384]{1,0:T(8,128)S(1)}, u32[]{:S(2)}, u32[]{:S(2)}) %collective-permute-start.2) | collective-permute-done | bytes 98336 | tf_op jit(solution)/shard_map/ppermute | solution.py:274
  80.5 0.9 add_convert_fusion.1
  81.4 7.8 %all_to_all.34 = bf16[4,64,384]{2,1,0:T(8,128)(2,1)S(1)} all-to-all(bf16[4,64,384]{2,1,0:T(8,128)(2,1)S(1)} %broadcast_in_dim.19), channel_id=1, replica_groups=mesh['z'=8,'y'=4,'core'=2,'tp'=4] {'y'}, dimensions={0} | all-to-all | bytes 393216 | tf_op jit(solution)/shard_map/all_to_all | solution.py:278
  89.3 0.8 broadcast_in_dim.20
  90.0 3.5 %all-to-all-start.5 = ((bf16[8,64,384]{2,1,0:T(8,128)(2,1)}), bf16[8,64,384]{2,1,0:T(8,128)(2,1)S(1)}, u32[]{:S(2)}, u32[]{:S(2)}) async-start(bf16[8,64,384]{2,1,0:T(8,128)(2,1)} %broadcast_in_dim.20), calls=%async_computation.5 | async-start | bytes 786432 | tf_op jit(solution)/shard_map/all_to_all | solution.py:278
  93.5 12.7 %all-to-all-done.5 = bf16[8,64,384]{2,1,0:T(8,128)(2,1)S(1)} async-done(((bf16[8,64,384]{2,1,0:T(8,128)(2,1)}), bf16[8,64,384]{2,1,0:T(8,128)(2,1)S(1)}, u32[]{:S(2)}, u32[]{:S(2)}) %all-to-all-start.5) | async-done | bytes 393248 | tf_op jit(solution)/shard_map/all_to_all | solution.py:278
  106.3 3.0 %collective-permute-start.3 = (bf16[64,384]{1,0:T(8,128)(2,1)S(1)}, bf16[64,384]{1,0:T(8,128)(2,1)S(1)}, u32[]{:S(2)}, u32[]{:S(2)}) collective-permute-start(bf16[64,384]{1,0:T(8,128)(2,1)S(1)} %add_convert_fusion), channel_id=1, source_target_pairs={{0,4},{4,0},{1,5},{5,1},{2,6},{6,2},{3,7},{7,3},{8,12},{12,8},{9,1... | collective-permute-start | bytes 147464 | tf_op jit(solution)/shard_map/ppermute | solution.py:274
  109.2 0.9 collective-permute-done.3
  (27 shorter events, 4.4 us)
Async XLA Ops:
  3.2 55.6 %copy-start.4 = (s32[128,8]{0,1:T(8,128)S(1)}, s32[128,8]{0,1:T(8,128)}, u32[]{:S(2)}) copy-start(s32[128,8]{0,1:T(8,128)} %param.25) | copy-start | bytes 12292
  3.2 56.3 %copy-start.5 = (f32[384]{0:T(512)S(1)}, f32[384]{0:T(512)}, u32[]{:S(2)}) copy-start(f32[384]{0:T(512)} %param.17) | copy-start | bytes 4612
  8.0 4.4 %collective-permute-start = (f32[128,256]{1,0:T(8,128)}, f32[128,256]{1,0:T(8,128)S(1)}, u32[]{:S(2)}, u32[]{:S(2)}) collective-permute-start(f32[128,256]{1,0:T(8,128)} %get-tuple-element.12), channel_id=1, source_target_pairs={{0,4},{4,0},{1,5},{5,1},{2,6},{6,2},{3,7},{7,3},{8,12},{12,8},{9,1... | collective-permute-start | bytes 393224 | tf_op jit(solution)/shard_map/ppermute | solution.py:274
  12.5 0.7 copy-start.2
  54.3 5.8 %copy-start = (bf16[16,32,256]{2,1,0:T(8,128)(2,1)}, bf16[16,32,256]{2,1,0:T(8,128)(2,1)S(1)}, u32[]{:S(2)}) copy-start(bf16[16,32,256]{2,1,0:T(8,128)(2,1)S(1)} %all_to_all.32.mine_ref) | copy-start | bytes 786436
  54.3 5.8 %collective-permute-start.1 = (bf16[16,32,256]{2,1,0:T(8,128)(2,1)S(1)}, bf16[16,32,256]{2,1,0:T(8,128)(2,1)S(1)}, u32[]{:S(2)}, u32[]{:S(2)}) collective-permute-start(bf16[16,32,256]{2,1,0:T(8,128)(2,1)S(1)} %all_to_all.32.mine_ref), channel_id=1, source_target_pairs={{0,4},{4,0},{1,5},{5,1},{2,6},{6,2},{3,7},{7,3},{8,12},{12,8},{9,1... | collective-permute-start | bytes 786440 | tf_op jit(solution)/shard_map/ppermute | solution.py:274
  60.1 0.7 copy-start.1
  64.7 41.6 %copy-start.3 = (f32[128,384]{1,0:T(8,128)S(1)}, f32[128,384]{1,0:T(8,128)}, u32[]{:S(2)}) copy-start(f32[128,384]{1,0:T(8,128)} %get-tuple-element.13) | copy-start | bytes 589828
  78.2 2.3 %collective-permute-start.2 = (f32[64,384]{1,0:T(8,128)}, f32[64,384]{1,0:T(8,128)S(1)}, u32[]{:S(2)}, u32[]{:S(2)}) collective-permute-start(f32[64,384]{1,0:T(8,128)} %get-tuple-element.16), channel_id=1, source_target_pairs={{0,4},{4,0},{1,5},{5,1},{2,6},{6,2},{3,7},{7,3},{8,12},{12,8},{9,1... | collective-permute-start | bytes 294920 | tf_op jit(solution)/shard_map/ppermute | solution.py:274
  90.0 16.1 %all-to-all-start.5 = ((bf16[8,64,384]{2,1,0:T(8,128)(2,1)}), bf16[8,64,384]{2,1,0:T(8,128)(2,1)S(1)}, u32[]{:S(2)}, u32[]{:S(2)}) async-start(bf16[8,64,384]{2,1,0:T(8,128)(2,1)} %broadcast_in_dim.20), calls=%async_computation.5 | async-start | bytes 786432 | tf_op jit(solution)/shard_map/all_to_all | solution.py:278
  106.3 3.9 %collective-permute-start.3 = (bf16[64,384]{1,0:T(8,128)(2,1)S(1)}, bf16[64,384]{1,0:T(8,128)(2,1)S(1)}, u32[]{:S(2)}, u32[]{:S(2)}) collective-permute-start(bf16[64,384]{1,0:T(8,128)(2,1)S(1)} %add_convert_fusion), channel_id=1, source_target_pairs={{0,4},{4,0},{1,5},{5,1},{2,6},{6,2},{3,7},{7,3},{8,12},{12,8},{9,1... | collective-permute-start | bytes 147464 | tf_op jit(solution)/shard_map/ppermute | solution.py:274

commit v2 on v1

--- a/solution.py
+++ b/solution.py
@@ -2,6 +2,7 @@
 
 import jax
 import jax.numpy as jnp
+import numpy as np
 from jax import lax
 from jax.experimental import pallas as pl
 from jax.experimental.pallas import tpu as pltpu
@@ -43,68 +44,91 @@
     return lax.dot_general(a, b, (((1,), (1,)), ((), ())), preferred_element_type=F32)
 
 
-def call(body, outs, n_in, smem=(), scratch=(), flops=10**7):
-    return pl.pallas_call(
+def call(body, outs, args, smem=(), scratch=(), flops=10**7):
+    outs = [pltpu.VMEM(shape, dtype) for shape, dtype in outs]
+    run = pl.pallas_call(
         body,
         out_shape=outs,
-        in_specs=[SMEM if i in smem else VMEM for i in range(n_in)],
-        out_specs=jax.tree.map(lambda _: VMEM, outs),
+        in_specs=[SMEM if i in smem else VMEM for i in range(len(args))],
+        out_specs=[VMEM for _ in outs],
         scratch_shapes=list(scratch),
         cost_estimate=pl.CostEstimate(flops=flops, bytes_accessed=10**6, transcendentals=0),
     )
-
-
-def attend_body(len_ref, tok_ref, gain_ref, w_ref, cos_ref, sin_ref, k_ref, v_ref, keep_ref, send_ref):
-    core = lax.axis_index("core")
-    seq = (lax.axis_index("z") * 4 + lax.axis_index("y")) * 2 + core
+    space = [pltpu.MemorySpace.SMEM if i in smem else pltpu.MemorySpace.VMEM for i in range(len(args))]
+    return run(*[pltpu.with_memory_space_constraint(a, m) for a, m in zip(args, space)])
+
+
+def cos_sin(angle):
+    turns = jnp.floor(angle * (2.0 / np.pi) + 0.5)
+    r = angle - turns * QUARTER[0]
+    r = r - turns * QUARTER[1]
+    r = r - turns * QUARTER[2]
+    r = r - turns * QUARTER[3]
+    r2 = r * r
+    sin = r + r * r2 * (-1.0 / 6 + r2 * (1.0 / 120 + r2 * (-1.0 / 5040 + r2 * (1.0 / 362880))))
+    cos = 1.0 - 0.5 * r2 + r2 * r2 * (1.0 / 24 + r2 * (-1.0 / 720 + r2 * (1.0 / 40320 - r2 * (1.0 / 3628800))))
+    which = turns.astype(jnp.int32) & 3
+    odd = (which & 1) == 1
+    c = jnp.where(odd, sin, cos)
+    s = jnp.where(odd, cos, sin)
+    return jnp.where((which == 1) | (which == 2), -c, c), jnp.where(which >= 2, -s, s)
+
+
+def quarter_pieces():
+    pieces = []
+    rest = np.pi / 2
+    for _ in range(3):
+        top = np.floor(rest * 2.0 ** (7 - np.floor(np.log2(rest)))) / 2.0 ** (7 - np.floor(np.log2(rest)))
+        pieces.append(float(top))
+        rest = rest - top
+    return pieces + [float(np.float32(rest))]
+
+
+QUARTER = quarter_pieces()
+
+
+def attend_body(len_ref, tok_ref, gain_ref, w_ref, freq_ref, k_ref, v_ref, out_ref):
+    seq = ((lax.axis_index("zh") * 2 + lax.axis_index("zl")) * 4 + lax.axis_index("y")) * 2 + lax.axis_index("core")
     x = tok_ref[...].astype(F32)
     normed = x * lax.rsqrt(jnp.mean(x * x, axis=-1, keepdims=True) + EPSILON) * gain_ref[...]
     proj = dot(normed.astype(BF16), w_ref[...])
-    cos = cos_ref[...]
-    sin = sin_ref[...]
-    lane = iota((TOKENS, 128), 1)
+    lane = iota((32, 128), 1)
+    row = iota((32, 128), 0)
     low = lane < 64
     first = (lane % 64) < 32
-    tiles = [proj[:, 128 * i : 128 * i + 128] for i in range(5)]
-
-    def rot(t):
-        swapped = jnp.where(first, pltpu.roll(t, 96, 1), pltpu.roll(t, 32, 1))
-        return t * cos + swapped * sin
-
-    turned = [rot(t) for t in tiles]
-    query = []
-    for g in range(2):
-        for q in range(GROUP):
-            at = g * 5 + q
-            t = turned[at // 2]
-            if at % 2 != g:
-                t = pltpu.roll(t, 64, 1)
-            query.append(jnp.where(low if g == 0 else ~low, t * 0.125, 0.0).astype(BF16))
-    key_new = jnp.where(low, pltpu.roll(turned[1], 64, 1), pltpu.roll(turned[4], 64, 1)).astype(BF16)
-    value_new = jnp.where(low, tiles[2], tiles[4]).astype(BF16)
-
-    row = iota((32, 256), 0)
-    col = iota((32, 256), 1)
-    same = (row // NEW) == (col // SLOTS)
-    slot = seq * SLOTS + col % SLOTS
+    slot = seq * SLOTS + lane % SLOTS
     nrow = iota((32, 32), 0)
     ncol = iota((32, 32), 1)
     ok_new = (nrow // NEW == ncol // NEW) & (ncol <= nrow) & (seq == 0)
-    glow = iota((32, 128), 1) < 64
-    glane = iota((32, 128), 1)
+    freq = freq_ref[...]
     for grp in range(4):
-        lens = jnp.zeros((32, 256), jnp.int32)
+        rows = slice(grp * 32, grp * 32 + 32)
+        lens = jnp.zeros((32, 128), jnp.int32)
         for r in range(8):
             lens = jnp.where(row // NEW == r, len_ref[grp * 8 + r], lens)
+        cos, sin = cos_sin((lens + row % NEW).astype(F32) * freq)
+        sin = jnp.where(first, -sin, sin)
+        tiles = [proj[rows, 128 * i : 128 * i + 128] for i in range(5)]
+        turned = [t * cos + jnp.where(first, pltpu.roll(t, 96, 1), pltpu.roll(t, 32, 1)) * sin for t in tiles]
+        query = []
+        for g in range(2):
+            for q in range(GROUP):
+                at = g * 5 + q
+                t = turned[at // 2]
+                if at % 2 != g:
+                    t = pltpu.roll(t, 64, 1)
+                query.append(jnp.where(low if g == 0 else ~low, t * 0.125, 0.0).astype(BF16))
+        qg = jnp.concatenate(query, axis=0)
+        key_new = jnp.where(low, pltpu.roll(turned[1], 64, 1), pltpu.roll(turned[4], 64, 1)).astype(BF16)
+        value_new = jnp.where(low, tiles[2], tiles[4]).astype(BF16)
+
         back = lens - 1 - slot
-        live = back >= 0
         safe = jnp.maximum(back, 0)
         age = safe - ((safe * 32833) >> 26) * WINDOW
-        ok = same & live & ((slot < SINK) | (age <= WINDOW - 1 - row % NEW))
-        rows = slice(grp * 32, grp * 32 + 32)
-        qg = jnp.concatenate([b[rows] for b in query], axis=0)
+        ok = (back >= 0) & ((slot < SINK) | (age <= WINDOW - 1 - row % NEW))
+        ok = jnp.concatenate([ok & (row // NEW == lane // SLOTS + 4 * i) for i in range(2)], axis=1)
         s = dot_t(qg, k_ref[grp * 256 : grp * 256 + 256, :]).reshape(6, 32, 256)
-        sn = dot_t(qg, key_new[rows]).reshape(6, 32, 32)
+        sn = dot_t(qg, key_new).reshape(6, 32, 32)
         s = jnp.where(ok[None], s, FLOOR_SCORE)
         sn = jnp.where(ok_new[None], sn, FLOOR_SCORE)
         m = jnp.maximum(jnp.max(s, axis=-1, keepdims=True), jnp.max(sn, axis=-1, keepdims=True))
@@ -112,24 +136,20 @@
         pn = jnp.where(ok_new[None], jnp.exp(sn - m), 0.0)
         mass = jnp.sum(p, axis=-1, keepdims=True) + jnp.sum(pn, axis=-1, keepdims=True)
         acc = dot(p.reshape(192, 256).astype(BF16), v_ref[grp * 256 : grp * 256 + 256, :]) + dot(
-            pn.reshape(192, 32).astype(BF16), value_new[rows]
+            pn.reshape(192, 32).astype(BF16), value_new
         )
         some = mass > 0.0
         mass = jnp.where(some, mass, 1.0)
         acc = acc.reshape(6, 32, 128) / mass
         lse = jnp.where(some, m + jnp.log(mass), FLOOR_SCORE)
-        packed = []
         for g in range(2):
             a = [acc[g * 3 + q] for q in range(3)]
             a = [b if q % 2 == g else pltpu.roll(b, 64, 1) for q, b in enumerate(a)]
             e = [lse[g * 3 + q] for q in range(3)]
-            stats = jnp.where(glane == 64, e[0], jnp.where(glane == 65, e[1], jnp.where(glane == 66, e[2], 0.0)))
-            packed.append((jnp.where(glow, a[0], a[1]), jnp.where(glow, a[2], stats)))
-        mine = core == 0
-        for i in range(2):
-            lanes = slice(128 * i, 128 * i + 128)
-            keep_ref[rows, lanes] = jnp.where(mine, packed[0][i], packed[1][i])
-            send_ref[rows, lanes] = jnp.where(mine, packed[1][i], packed[0][i])
+            stats = jnp.where(lane == 64, e[0], jnp.where(lane == 65, e[1], jnp.where(lane == 66, e[2], 0.0)))
+            lo, hi = encode(jnp.where(low, a[0], a[1]), a[2], stats)
+            out_ref[grp * 2 + g, :, :128] = lo
+            out_ref[grp * 2 + g, :, 128:] = hi
 
 
 def merge(parts):
@@ -163,19 +183,8 @@
     return lo, hi, jnp.where((lane >= 64) & (lane < 67), lse, 0.0)
 
 
-def merge_core_body(keep_ref, got_ref, out_ref):
-    lane = iota((TOKENS, 128), 1)
-    parts = []
-    for ref in (keep_ref, got_ref):
-        hi = ref[:, 128:]
-        parts.append((ref[:, :128], hi, jnp.where(lane >= 64, hi, 0.0)))
-    lo, hi = encode(*merge(parts))
-    out_ref[:, :128] = lo
-    out_ref[:, 128:] = hi
-
-
 def merge_y_body(in_ref, out_ref):
-    lo, hi = encode(*merge([decode(in_ref[i]) for i in range(4)]))
+    lo, hi = encode(*merge([decode(in_ref[i]) for i in range(8)]))
     for i in range(8):
         out_ref[i, :, :128] = lo
         out_ref[i, :, 128:] = hi
@@ -213,7 +222,7 @@
     g0, g1, g2 = split3(gained)
     logits = dot_t(g0, router) + dot_t(g1, router) + dot_t(g2, router)
     both = jnp.concatenate([dot_t(g0, gate_ref[...]), dot_t(g0, up_ref[...])], axis=1)
-    routes = routes_ref[...]
+    routes = routes_ref[...].T
     expert = (iota((TOKENS, 640), 1) % 320) // FF
     elane = iota((TOKENS, EXPERTS), 1)
     lane = iota((TOKENS, 128), 1)
@@ -257,7 +266,7 @@
     ecol = iota((128, 1024), 1)
     spread_to = ((erow % FF == ecol % FF) & (erow // FF == ecol // 128)).astype(BF16)
     tiled = dot(scaled, spread_to)
-    routes = routes_ref[...]
+    routes = routes_ref[...].T
     spread = []
     for i in range(3):
         s = jnp.zeros((TOKENS, 128), F32)
@@ -294,55 +303,54 @@
     routes,
 ):
     core = lax.axis_index("core")
-    sds = jax.ShapeDtypeStruct
-    places = (lengths[:, None] + jnp.arange(NEW, dtype=jnp.int32)[None, :]).reshape(TOKENS).astype(F32)
+    z = ("zh", "zl")
     half = HEAD // 2
-    freqs = jnp.exp(-jnp.log(ROPE_BASE) * jnp.arange(half, dtype=F32) / half)
-    angles = places[:, None] * jnp.tile(freqs, 4)[None, :]
-    cos = jnp.cos(angles)
-    sin = jnp.where(jnp.arange(128)[None, :] % 64 < half, -jnp.sin(angles), jnp.sin(angles))
-
-    keep, send = call(attend_body, (sds((TOKENS, 256), F32),) * 2, 8, smem=(0,))(
-        lengths,
-        tokens,
-        attn_gain.reshape(1, D),
-        qkv_weight,
-        cos,
-        sin,
-        cache_keys.reshape(REQS * SLOTS, 128),
-        cache_values.reshape(REQS * SLOTS, 128),
-    )
-    packed = call(merge_core_body, sds((TOKENS, 256), BF16), 2)(keep, swap(send))
-    packed = exchange(packed.reshape(4, 32, 256), "y")
-    packed = call(merge_y_body, sds((8, 32, 256), BF16), 1)(packed)
-    packed = exchange(packed, "z")
-    packed = call(merge_z_body, sds((16, 32, 256), BF16), 1)(packed)
+    freqs = np.tile(np.exp(-np.log(ROPE_BASE) * np.arange(half) / half), 4).astype(np.float32)
+    (packed,) = call(
+        attend_body,
+        [((8, 32, 256), BF16)],
+        (
+            lengths,
+            tokens,
+            attn_gain.reshape(1, D),
+            qkv_weight,
+            jnp.asarray(freqs[None, :]),
+            cache_keys.reshape(REQS * SLOTS, 128),
+            cache_values.reshape(REQS * SLOTS, 128),
+        ),
+        smem=(0,),
+    )
+    (packed,) = call(merge_y_body, [((8, 32, 256), BF16)], (exchange(packed, ("y", "core")),))
+    (packed,) = call(merge_z_body, [((16, 32, 256), BF16)], (exchange(packed, z),))
     mine = exchange(packed, ("y", "tp"))
     other = swap(mine)
 
-    residual, picked = call(project_body, (sds((TOKENS, FEAT), F32), sds((4, TOKENS, 256), BF16)), 9)(
-        mine,
-        other,
-        tokens,
-        out_weight,
-        moe_gain.reshape(1, FEAT),
-        router_weight.T,
-        expert_gate.transpose(0, 2, 1).reshape(EXPERTS * FF, FEAT),
-        expert_up.transpose(0, 2, 1).reshape(EXPERTS * FF, FEAT),
-        routes,
-    )
-    picked = exchange(picked, "tp")
+    residual, picked = call(
+        project_body,
+        [((TOKENS, FEAT), F32), ((4, TOKENS, 256), BF16)],
+        (
+            mine,
+            other,
+            tokens,
+            out_weight,
+            moe_gain.reshape(1, FEAT),
+            router_weight.T,
+            expert_gate.transpose(0, 2, 1).reshape(EXPERTS * FF, FEAT),
+            expert_up.transpose(0, 2, 1).reshape(EXPERTS * FF, FEAT),
+            routes.T,
+        ),
+    )
     keep, send = call(
         expert_body,
-        (sds((TOKENS // 2, FEAT), F32),) * 2,
-        3,
+        [((TOKENS // 2, FEAT), F32)] * 2,
+        (exchange(picked, "tp"), routes.T, expert_down.reshape(EXPERTS * FF, FEAT)),
         scratch=[pltpu.VMEM((TOKENS, FEAT), F32)],
-    )(picked, routes, expert_down.reshape(EXPERTS * FF, FEAT))
+    )
 
     part = (keep + swap(send)).astype(BF16)
-    part = exchange(jnp.broadcast_to(part, (4,) + part.shape), "y")
+    part = exchange(jnp.broadcast_to(part, (8,) + part.shape), ("zl", "y"))
     part = jnp.sum(part.astype(F32), axis=0).astype(BF16)
-    part = exchange(jnp.broadcast_to(part, (8,) + part.shape), "z")
+    part = exchange(jnp.broadcast_to(part, (4,) + part.shape), "zh")
     own = lax.dynamic_slice_in_dim(residual, core * (TOKENS // 2), TOKENS // 2, 0)
     own = (own + jnp.sum(part.astype(F32), axis=0)).astype(BF16)
     theirs = swap(own)
@@ -351,8 +359,8 @@
 
 
 def solution(mesh):
-    seq = ("z", "y", "core")
-    grid = Mesh(mesh.devices.reshape(8, 4, 2, 4), seq + ("tp",))
+    seq = ("zh", "zl", "y", "core")
+    grid = Mesh(mesh.devices.reshape(4, 2, 4, 2, 4), seq + ("tp",))
     in_specs = (
         P(),
         P(),

time: 112 us -> 97.6 us (0.87)
  Pallas kernels: 17 us -> 6.47 us
  waiting for transfers between devices: 15.9 us -> 10.6 us
  local copies, waits for them, and re-layouts: 4.93 us -> 9.38 us
  blocking collectives: 54.2 us -> 58.3 us
  starting transfers between devices: 15.3 us -> 11.3 us
  other arithmetic: 3.39 us -> 0.78 us
    pallas_call x6 -> x5, Pallas kernels: 17 us -> 6.47 us  [call(): run(*[pltpu.with_memory_space_constraint(a, m) for a, m in zip(args, spac...]
    unnamed x13 -> x26, local copies, waits for them, and re-layouts: 2.08 us -> 7.94 us
    all_to_all x1, waiting for transfers between devices: 12.7 us -> 7.66 us  [exchange(): return lax.all_to_all(v, axes, 0, 0, tiled=True)]
    all_to_all x5, blocking collectives: 54.2 us -> 58.3 us  [exchange(): return lax.all_to_all(v, axes, 0, 0, tiled=True)]
    ppermute x4 -> x3, starting transfers between devices: 11.9 us -> 7.9 us  [swap(): return lax.ppermute(v, 'core', [(0, 1), (1, 0)])]
    ppermute x4 -> x3, waiting for transfers between devices: 3.24 us -> 2.98 us  [swap(): return lax.ppermute(v, 'core', [(0, 1), (1, 0)])]
  transfers between devices with their start and end apart: 5 -> 4, of which waited for: 4 -> 4; matrix products, arithmetic and copies ran while one was open for 1% -> 0% of each run, Pallas kernels for 0% -> 0%
where the time goes in v2:
time: 97.6 us; the launch traced here: 97 us
  blocking collectives  58.3 us (60%)
  starting transfers between devices  11.3 us (12%)
  waiting for transfers between devices  10.6 us (11%)
  local copies, waits for them, and re-layouts  9.38 us (10%)
  Pallas kernels  6.47 us (7%)
    all_to_all x5, blocking collectives, exchange(): return lax.all_to_all(v, axes, 0, 0, tiled=True)  58.3 us
    unnamed x26, local copies, waits for them, and re-layouts  7.94 us
    ppermute x3, starting transfers between devices, swap(): return lax.ppermute(v, 'core', [(0, 1), (1, 0)])  7.9 us
    all_to_all x1, waiting for transfers between devices, exchange(): return lax.all_to_all(v, axes, 0, 0, tiled=True)  7.66 us
    pallas_call x5, Pallas kernels, call(): run(*[pltpu.with_memory_space_constraint(a, m) for a, m in zip(args, spac...  6.47 us
    all_to_all x1, starting transfers between devices, exchange(): return lax.all_to_all(v, axes, 0, 0, tiled=True)  3.36 us
    ppermute x3, waiting for transfers between devices, swap(): return lax.ppermute(v, 'core', [(0, 1), (1, 0)])  2.98 us
  transfers between devices with their start and end apart: 4, of which 4 were waited for; matrix products, arithmetic and copies ran while one was open for 0% of the time, Pallas kernels for 0%

profile of v2, /device:TPU:1, one launch (start us, length us, event | category | flops | bytes accessed | tf_op | source)
XLA Modules:
  0.0 97.0 jit_solution(658386214587559975)
XLA Ops:
  0.0 0.7 reshape.21.gain_ref
  0.7 1.5 %copy-done = bf16[1536,640]{1,0:T(8,128)(2,1)S(1)} copy-done((bf16[1536,640]{1,0:T(8,128)(2,1)S(1)}, bf16[1536,640]{1,0:T(8,128)(2,1)}, u32[]{:S(2)}) %copy-start) | copy-done | bytes 1966104
  2.2 1.0 %copy-done.1 = bf16[128,1536]{1,0:T(8,128)(2,1)S(1)} copy-done((bf16[128,1536]{1,0:T(8,128)(2,1)S(1)}, bf16[128,1536]{1,0:T(8,128)(2,1)}, u32[]{:S(2)}) %copy-start.1) | copy-done | bytes 393240
  3.2 0.9 copy-done.4
  4.2 0.9 copy-done.5
  5.8 3.1 %shard_map.136 = bf16[8,32,256]{2,1,0:T(8,128)(2,1)S(1)} custom-call(s32[32]{0:T(128)} %len_ref.1, bf16[128,1536]{1,0:T(8,128)(2,1)S(1)} %copy-done.1, f32[1,1536]{1,0:T(1,128)S(1)} %reshape.21.gain_ref, bf16[1536,640]{1,0:T(8,128)(2,1)S(1)} %copy-done, f32[1,128]{1,0:T(1,128)S(1)} %copy-done.11, bf16[1024,128]{1,0:T(8,128)(2,1)S(1)} %bitcast.11, ...), custom_call_target="tpu_custom_call" | custom-call | flops 10000000 | bytes 1000000 | tf_op jit(solution)/shard_map/pallas_call | solution.py:58
  8.9 11.2 %all_to_all.30.in_ref = bf16[8,32,256]{2,1,0:T(8,128)(2,1)S(1)} all-to-all(bf16[8,32,256]{2,1,0:T(8,128)(2,1)S(1)} %shard_map.136), channel_id=1, replica_groups=mesh['zh'=4,'zl'=2,'y'=4,'core'=2,'tp'=4] {'y','core'}, dimensions={0} | all-to-all | bytes 262144 | tf_op jit(solution)/shard_map/all_to_all | solution.py:287
  20.5 15.8 %all_to_all.31.in_ref = bf16[8,32,256]{2,1,0:T(8,128)(2,1)S(1)} all-to-all(bf16[8,32,256]{2,1,0:T(8,128)(2,1)S(1)} %shard_map.137), channel_id=1, replica_groups=mesh['zh'=4,'zl'=2,'y'=4,'core'=2,'tp'=4] {'zh','zl'}, dimensions={0} | all-to-all | bytes 262144 | tf_op jit(solution)/shard_map/all_to_all | solution.py:287
  36.7 12.2 %all_to_all.32.mine_ref = bf16[16,32,256]{2,1,0:T(8,128)(2,1)S(1)} all-to-all(bf16[16,32,256]{2,1,0:T(8,128)(2,1)S(1)} %shard_map.138), channel_id=1, replica_groups=mesh['zh'=4,'zl'=2,'y'=4,'core'=2,'tp'=4] {'y','tp'}, dimensions={0} | all-to-all | bytes 524288 | tf_op jit(solution)/shard_map/all_to_all | solution.py:287
  48.8 3.7 %collective-permute-start = (bf16[16,32,256]{2,1,0:T(8,128)(2,1)S(1)}, bf16[16,32,256]{2,1,0:T(8,128)(2,1)S(1)}, u32[]{:S(2)}, u32[]{:S(2)}) collective-permute-start(bf16[16,32,256]{2,1,0:T(8,128)(2,1)S(1)} %all_to_all.32.mine_ref), channel_id=1, source_target_pairs={{0,4},{4,0},{1,5},{5,1},{2,6},{6,2},{3,7},{7,3},{8,12},{12,8},{9,1... | collective-permute-start | bytes 786440 | tf_op jit(solution)/shard_map/ppermute | solution.py:283
  52.5 1.2 %collective-permute-done.other_ref = bf16[16,32,256]{2,1,0:T(8,128)(2,1)S(1)} collective-permute-done((bf16[16,32,256]{2,1,0:T(8,128)(2,1)S(1)}, bf16[16,32,256]{2,1,0:T(8,128)(2,1)S(1)}, u32[]{:S(2)}, u32[]{:S(2)}) %collective-permute-start) | collective-permute-done | bytes 262176 | tf_op jit(solution)/shard_map/ppermute | solution.py:283
  53.7 0.9 copy-done.6
  54.7 0.9 copy-done.7
  55.6 1.5 %shard_map.139 = (f32[128,384]{1,0:T(8,128)S(1)}, bf16[4,128,256]{2,1,0:T(8,128)(2,1)S(1)}) custom-call(bf16[16,32,256]{2,1,0:T(8,128)(2,1)S(1)} %all_to_all.32.mine_ref, bf16[16,32,256]{2,1,0:T(8,128)(2,1)S(1)} %collective-permute-done.other_ref, bf16[128,1536]{1,0:T(8,128)(2,1)S(1)} %copy-done.2, bf16[1536,384]{1,0:T(8,128)(2,1)S(1)} %copy-done.3, ...), custom_call_target="tpu_custom_call" | custom-call | flops 10000000 | bytes 1000000 | tf_op jit(solution)/shard_map/pallas_call | solution.py:58
  57.1 8.8 %all_to_all.33.in_ref = bf16[4,128,256]{2,1,0:T(8,128)(2,1)S(1)} all-to-all(bf16[4,128,256]{2,1,0:T(8,128)(2,1)S(1)} %get-tuple-element.10), channel_id=1, replica_groups=mesh['zh'=4,'zl'=2,'y'=4,'core'=2,'tp'=4] {'tp'}, dimensions={0} | all-to-all | bytes 524288 | tf_op jit(solution)/shard_map/all_to_all | solution.py:287
  65.9 0.9 copy-done.8
  66.8 1.2 %shard_map.140 = (f32[64,384]{1,0:T(8,128)S(1)}, f32[64,384]{1,0:T(8,128)S(1)}) custom-call(bf16[4,128,256]{2,1,0:T(8,128)(2,1)S(1)} %all_to_all.33.in_ref, s32[8,128]{1,0:T(8,128)S(1)} %bitcast.18, bf16[320,384]{1,0:T(8,128)(2,1)S(1)} %bitcast.15), custom_call_target="tpu_custom_call" | custom-call | flops 10000000 | bytes 1000000 | tf_op jit(solution)/shard_map/pallas_call | solution.py:58
  68.0 1.3 %collective-permute-start.1 = (f32[64,384]{1,0:T(8,128)S(1)}, f32[64,384]{1,0:T(8,128)S(1)}, u32[]{:S(2)}, u32[]{:S(2)}) collective-permute-start(f32[64,384]{1,0:T(8,128)S(1)} %get-tuple-element.12), channel_id=1, source_target_pairs={{0,4},{4,0},{1,5},{5,1},{2,6},{6,2},{3,7},{7,3},{8,12},{12,8},{9,1... | collective-permute-start | bytes 294920 | tf_op jit(solution)/shard_map/ppermute | solution.py:283
  69.3 0.9 collective-permute-done.1
  70.3 10.3 %all_to_all.34 = bf16[8,64,384]{2,1,0:T(8,128)(2,1)S(1)} all-to-all(bf16[8,64,384]{2,1,0:T(8,128)(2,1)S(1)} %broadcast_in_dim.6), channel_id=1, replica_groups=mesh['zh'=4,'zl'=2,'y'=4,'core'=2,'tp'=4] {'zl','y'}, dimensions={0} | all-to-all | bytes 786432 | tf_op jit(solution)/shard_map/all_to_all | solution.py:287
  81.4 3.4 %all-to-all-start.5 = ((bf16[4,64,384]{2,1,0:T(8,128)(2,1)}), bf16[4,64,384]{2,1,0:T(8,128)(2,1)S(1)}, u32[]{:S(2)}, u32[]{:S(2)}) async-start(bf16[4,64,384]{2,1,0:T(8,128)(2,1)} %broadcast_in_dim.7), calls=%async_computation.5 | async-start | bytes 393216 | tf_op jit(solution)/shard_map/all_to_all | solution.py:287
  84.8 7.7 %all-to-all-done.5 = bf16[4,64,384]{2,1,0:T(8,128)(2,1)S(1)} async-done(((bf16[4,64,384]{2,1,0:T(8,128)(2,1)}), bf16[4,64,384]{2,1,0:T(8,128)(2,1)S(1)}, u32[]{:S(2)}, u32[]{:S(2)}) %all-to-all-start.5) | async-done | bytes 196640 | tf_op jit(solution)/shard_map/all_to_all | solution.py:287
  92.5 2.9 %collective-permute-start.2 = (bf16[64,384]{1,0:T(8,128)(2,1)S(1)}, bf16[64,384]{1,0:T(8,128)(2,1)S(1)}, u32[]{:S(2)}, u32[]{:S(2)}) collective-permute-start(bf16[64,384]{1,0:T(8,128)(2,1)S(1)} %add_convert_fusion), channel_id=1, source_target_pairs={{0,4},{4,0},{1,5},{5,1},{2,6},{6,2},{3,7},{7,3},{8,12},{12,8},{9,1... | collective-permute-start | bytes 147464 | tf_op jit(solution)/shard_map/ppermute | solution.py:283
  95.4 0.9 collective-permute-done.2
  (30 shorter events, 2.9 us)
Async XLA Ops:
  0.7 1.5 %copy-start = (bf16[1536,640]{1,0:T(8,128)(2,1)S(1)}, bf16[1536,640]{1,0:T(8,128)(2,1)}, u32[]{:S(2)}) copy-start(bf16[1536,640]{1,0:T(8,128)(2,1)} %w_ref.2) | copy-start | bytes 5898244
  2.2 1.0 %copy-start.1 = (bf16[128,1536]{1,0:T(8,128)(2,1)S(1)}, bf16[128,1536]{1,0:T(8,128)(2,1)}, u32[]{:S(2)}) copy-start(bf16[128,1536]{1,0:T(8,128)(2,1)} %tok_ref.3) | copy-start | bytes 1179652
  3.2 0.9 copy-start.4
  4.2 0.9 copy-start.5
  5.1 0.7 copy-start.11
  5.8 46.7 %copy-start.12 = (f32[384]{0:T(512)S(1)}, f32[384]{0:T(512)}, u32[]{:S(2)}) copy-start(f32[384]{0:T(512)} %param.18) | copy-start | bytes 4612
  5.8 47.9 %copy-start.2 = (bf16[128,1536]{1,0:T(8,128)(2,1)S(1)}, bf16[128,1536]{1,0:T(8,128)(2,1)}, u32[]{:S(2)}) copy-start(bf16[128,1536]{1,0:T(8,128)(2,1)} %tok_ref.3) | copy-start | bytes 1179652
  5.8 47.9 %copy-start.9 = (bf16[384,40]{0,1:T(8,128)(2,1)S(1)}, bf16[384,40]{0,1:T(8,128)(2,1)}, u32[]{:S(2)}) copy-start(bf16[384,40]{0,1:T(8,128)(2,1)} %param.19) | copy-start | bytes 92164
  5.8 47.9 %copy-start.10 = (s32[128,8]{0,1:T(8,128)S(1)}, s32[128,8]{0,1:T(8,128)}, u32[]{:S(2)}) copy-start(s32[128,8]{0,1:T(8,128)} %param.26) | copy-start | bytes 12292
  8.9 44.8 %copy-start.3 = (bf16[1536,384]{1,0:T(8,128)(2,1)S(1)}, bf16[1536,384]{1,0:T(8,128)(2,1)}, u32[]{:S(2)}) copy-start(bf16[1536,384]{1,0:T(8,128)(2,1)} %w_ref.3) | copy-start | bytes 3538948
  48.8 4.8 %collective-permute-start = (bf16[16,32,256]{2,1,0:T(8,128)(2,1)S(1)}, bf16[16,32,256]{2,1,0:T(8,128)(2,1)S(1)}, u32[]{:S(2)}, u32[]{:S(2)}) collective-permute-start(bf16[16,32,256]{2,1,0:T(8,128)(2,1)S(1)} %all_to_all.32.mine_ref), channel_id=1, source_target_pairs={{0,4},{4,0},{1,5},{5,1},{2,6},{6,2},{3,7},{7,3},{8,12},{12,8},{9,1... | collective-permute-start | bytes 786440 | tf_op jit(solution)/shard_map/ppermute | solution.py:283
  53.7 0.9 copy-start.6
  54.7 0.9 copy-start.7
  65.9 0.9 copy-start.8
  68.0 2.2 %collective-permute-start.1 = (f32[64,384]{1,0:T(8,128)S(1)}, f32[64,384]{1,0:T(8,128)S(1)}, u32[]{:S(2)}, u32[]{:S(2)}) collective-permute-start(f32[64,384]{1,0:T(8,128)S(1)} %get-tuple-element.12), channel_id=1, source_target_pairs={{0,4},{4,0},{1,5},{5,1},{2,6},{6,2},{3,7},{7,3},{8,12},{12,8},{9,1... | collective-permute-start | bytes 294920 | tf_op jit(solution)/shard_map/ppermute | solution.py:283
  81.4 11.0 %all-to-all-start.5 = ((bf16[4,64,384]{2,1,0:T(8,128)(2,1)}), bf16[4,64,384]{2,1,0:T(8,128)(2,1)S(1)}, u32[]{:S(2)}, u32[]{:S(2)}) async-start(bf16[4,64,384]{2,1,0:T(8,128)(2,1)} %broadcast_in_dim.7), calls=%async_computation.5 | async-start | bytes 393216 | tf_op jit(solution)/shard_map/all_to_all | solution.py:287
  92.5 3.8 %collective-permute-start.2 = (bf16[64,384]{1,0:T(8,128)(2,1)S(1)}, bf16[64,384]{1,0:T(8,128)(2,1)S(1)}, u32[]{:S(2)}, u32[]{:S(2)}) collective-permute-start(bf16[64,384]{1,0:T(8,128)(2,1)S(1)} %add_convert_fusion), channel_id=1, source_target_pairs={{0,4},{4,0},{1,5},{5,1},{2,6},{6,2},{3,7},{7,3},{8,12},{12,8},{9,1... | collective-permute-start | bytes 147464 | tf_op jit(solution)/shard_map/ppermute | solution.py:283

commit v3 on v2

--- a/solution.py
+++ b/solution.py
@@ -21,6 +21,7 @@
 SLOTS = 32
 FEAT = 384
 FF = 8
+CHUNKS = 4
 
 EPSILON = 1e-06
 ROPE_BASE = 10000.0
@@ -44,18 +45,25 @@
     return lax.dot_general(a, b, (((1,), (1,)), ((), ())), preferred_element_type=F32)
 
 
-def call(body, outs, args, smem=(), scratch=(), flops=10**7):
-    outs = [pltpu.VMEM(shape, dtype) for shape, dtype in outs]
+def call(body, outs, args, smem=(), raw=(), scratch=(), pinned=True):
+    kinds = ["s" if i in smem else "r" if i in raw else "v" for i in range(len(args))]
     run = pl.pallas_call(
         body,
-        out_shape=outs,
-        in_specs=[SMEM if i in smem else VMEM for i in range(len(args))],
+        out_shape=[(pltpu.VMEM if pinned else jax.ShapeDtypeStruct)(shape, dtype) for shape, dtype in outs],
+        in_specs=[{"s": SMEM, "r": pl.BlockSpec(memory_space=pl.ANY), "v": VMEM}[k] for k in kinds],
         out_specs=[VMEM for _ in outs],
         scratch_shapes=list(scratch),
-        cost_estimate=pl.CostEstimate(flops=flops, bytes_accessed=10**6, transcendentals=0),
+        cost_estimate=pl.CostEstimate(flops=10**7, bytes_accessed=10**6, transcendentals=0),
     )
-    space = [pltpu.MemorySpace.SMEM if i in smem else pltpu.MemorySpace.VMEM for i in range(len(args))]
-    return run(*[pltpu.with_memory_space_constraint(a, m) for a, m in zip(args, space)])
+    space = {"s": pltpu.MemorySpace.SMEM, "r": pl.ANY, "v": pltpu.MemorySpace.VMEM}
+    return run(*[pltpu.with_memory_space_constraint(a, space[k]) for a, k in zip(args, kinds)])
+
+
+def started(pairs, sems):
+    copies = [pltpu.make_async_copy(src, dst, sems.at[i]) for i, (src, dst) in enumerate(pairs)]
+    for c in copies:
+        c.start()
+    return copies
 
 
 def cos_sin(angle):
@@ -87,11 +95,44 @@
 QUARTER = quarter_pieces()
 
 
-def attend_body(len_ref, tok_ref, gain_ref, w_ref, freq_ref, k_ref, v_ref, out_ref):
+def attend_body(
+    len_ref,
+    tok_hbm,
+    gain_hbm,
+    w_hbm,
+    k_hbm,
+    v_hbm,
+    out_ref,
+    tok_ref,
+    gain_ref,
+    w_ref,
+    k_ref,
+    v_ref,
+    sems,
+):
+    part = D // CHUNKS
+    pairs = [(tok_hbm, tok_ref), (gain_hbm, gain_ref)]
+    pairs += [(w_hbm.at[pl.ds(i * part, part)], w_ref.at[pl.ds(i * part, part)]) for i in range(CHUNKS)]
+    pairs += [(k_hbm, k_ref), (v_hbm, v_ref)]
+    copies = started(pairs, sems)
     seq = ((lax.axis_index("zh") * 2 + lax.axis_index("zl")) * 4 + lax.axis_index("y")) * 2 + lax.axis_index("core")
+    half = HEAD // 2
+    spot = iota((8, 128), 1) % half
+    freq = jnp.zeros((8, 128), F32)
+    for i in range(half):
+        freq = jnp.where(spot == i, float(np.float32(ROPE_BASE ** (-i / half))), freq)
+    freq = freq[:1]
+    copies[0].wait()
+    copies[1].wait()
     x = tok_ref[...].astype(F32)
-    normed = x * lax.rsqrt(jnp.mean(x * x, axis=-1, keepdims=True) + EPSILON) * gain_ref[...]
-    proj = dot(normed.astype(BF16), w_ref[...])
+    normed = x * lax.rsqrt(jnp.mean(x * x, axis=-1, keepdims=True) + EPSILON) * gain_ref[...].reshape(1, D)
+    normed = normed.astype(BF16)
+    proj = jnp.zeros((TOKENS, 640), F32)
+    for i in range(CHUNKS):
+        copies[2 + i].wait()
+        proj = proj + dot(normed[:, i * part : (i + 1) * part], w_ref[i * part : (i + 1) * part, :])
+    copies[2 + CHUNKS].wait()
+    copies[3 + CHUNKS].wait()
     lane = iota((32, 128), 1)
     row = iota((32, 128), 0)
     low = lane < 64
@@ -100,7 +141,6 @@
     nrow = iota((32, 32), 0)
     ncol = iota((32, 32), 1)
     ok_new = (nrow // NEW == ncol // NEW) & (ncol <= nrow) & (seq == 0)
-    freq = freq_ref[...]
     for grp in range(4):
         rows = slice(grp * 32, grp * 32 + 32)
         lens = jnp.zeros((32, 128), jnp.int32)
@@ -206,7 +246,23 @@
     return a, b, (r - b.astype(F32)).astype(BF16)
 
 
-def project_body(mine_ref, other_ref, tok_ref, w_ref, gain_ref, router_ref, gate_ref, up_ref, routes_ref, res_ref, out_ref):
+def project_body(
+    mine_ref,
+    other_ref,
+    tok_ref,
+    w_ref,
+    gain_ref,
+    router_ref,
+    gate_hbm,
+    up_hbm,
+    routes_ref,
+    res_ref,
+    out_ref,
+    gate_ref,
+    up_ref,
+    sems,
+):
+    copies = started([(gate_hbm, gate_ref), (up_hbm, up_ref)], sems)
     core = lax.axis_index("core")
     tp = lax.axis_index("tp")
     acc = tok_ref[:, pl.ds(pl.multiple_of(tp * FEAT, 128), FEAT)].astype(F32)
@@ -221,6 +277,8 @@
     router = router_ref[...]
     g0, g1, g2 = split3(gained)
     logits = dot_t(g0, router) + dot_t(g1, router) + dot_t(g2, router)
+    for c in copies:
+        c.wait()
     both = jnp.concatenate([dot_t(g0, gate_ref[...]), dot_t(g0, up_ref[...])], axis=1)
     routes = routes_ref[...].T
     expert = (iota((TOKENS, 640), 1) % 320) // FF
@@ -245,7 +303,8 @@
         out_ref[i, :, 128:] = tail
 
 
-def expert_body(in_ref, routes_ref, down_ref, keep_ref, send_ref, part_ref):
+def expert_body(in_ref, routes_ref, down_hbm, keep_ref, send_ref, part_ref, down_ref, sems):
+    copies = started([(down_hbm, down_ref)], sems)
     core = lax.axis_index("core")
     lane = iota((TOKENS, 128), 1)
     picks = sum(in_ref[i, :, :128].astype(F32) for i in range(4))
@@ -274,9 +333,34 @@
             s = jnp.where(lane // FF + 16 * i == routes[:, k : k + 1], tiled[:, 128 * k : 128 * k + 128], s)
         spread.append(s)
     spread = jnp.concatenate(spread, axis=1)[:, :320].astype(BF16)
+    copies[0].wait()
     part_ref[...] = dot(spread, down_ref[...])
     keep_ref[...] = part_ref[pl.ds(pl.multiple_of(core * 64, 64), 64), :]
     send_ref[...] = part_ref[pl.ds(pl.multiple_of((1 - core) * 64, 64), 64), :]
+
+
+def pair_body(keep_ref, got_ref, out_ref):
+    v = (keep_ref[...] + got_ref[...]).astype(BF16)
+    for i in range(8):
+        out_ref[i] = v
+
+
+def group_body(in_ref, out_ref):
+    v = sum(in_ref[i].astype(F32) for i in range(8)).astype(BF16)
+    for i in range(4):
+        out_ref[i] = v
+
+
+def finish_body(in_ref, res_ref, out_ref):
+    core = lax.axis_index("core")
+    own = res_ref[pl.ds(pl.multiple_of(core * 64, 64), 64), :]
+    out_ref[...] = (own + sum(in_ref[i].astype(F32) for i in range(4))).astype(BF16)
+
+
+def assemble_body(own_ref, other_ref, out_ref):
+    core = lax.axis_index("core")
+    out_ref[pl.ds(pl.multiple_of(core * 64, 64), 64), :] = own_ref[...]
+    out_ref[pl.ds(pl.multiple_of((1 - core) * 64, 64), 64), :] = other_ref[...]
 
 
 def swap(v):
@@ -302,23 +386,29 @@
     lengths,
     routes,
 ):
-    core = lax.axis_index("core")
     z = ("zh", "zl")
-    half = HEAD // 2
-    freqs = np.tile(np.exp(-np.log(ROPE_BASE) * np.arange(half) / half), 4).astype(np.float32)
+    units = EXPERTS * FF
     (packed,) = call(
         attend_body,
         [((8, 32, 256), BF16)],
         (
             lengths,
             tokens,
-            attn_gain.reshape(1, D),
+            attn_gain,
             qkv_weight,
-            jnp.asarray(freqs[None, :]),
             cache_keys.reshape(REQS * SLOTS, 128),
             cache_values.reshape(REQS * SLOTS, 128),
         ),
         smem=(0,),
+        raw=range(1, 6),
+        scratch=[
+            pltpu.VMEM((TOKENS, D), BF16),
+            pltpu.VMEM((D,), F32),
+            pltpu.VMEM((D, 640), BF16),
+            pltpu.VMEM((REQS * SLOTS, 128), BF16),
+            pltpu.VMEM((REQS * SLOTS, 128), BF16),
+            pltpu.SemaphoreType.DMA((4 + CHUNKS,)),
+        ],
     )
     (packed,) = call(merge_y_body, [((8, 32, 256), BF16)], (exchange(packed, ("y", "core")),))
     (packed,) = call(merge_z_body, [((16, 32, 256), BF16)], (exchange(packed, z),))
@@ -335,27 +425,26 @@
             out_weight,
             moe_gain.reshape(1, FEAT),
             router_weight.T,
-            expert_gate.transpose(0, 2, 1).reshape(EXPERTS * FF, FEAT),
-            expert_up.transpose(0, 2, 1).reshape(EXPERTS * FF, FEAT),
+            expert_gate.transpose(0, 2, 1).reshape(units, FEAT),
+            expert_up.transpose(0, 2, 1).reshape(units, FEAT),
             routes.T,
         ),
+        raw=(6, 7),
+        scratch=[pltpu.VMEM((units, FEAT), BF16)] * 2 + [pltpu.SemaphoreType.DMA((2,))],
     )
+    half = ((TOKENS // 2, FEAT), F32)
     keep, send = call(
         expert_body,
-        [((TOKENS // 2, FEAT), F32)] * 2,
-        (exchange(picked, "tp"), routes.T, expert_down.reshape(EXPERTS * FF, FEAT)),
-        scratch=[pltpu.VMEM((TOKENS, FEAT), F32)],
+        [half, half],
+        (exchange(picked, "tp"), routes.T, expert_down.reshape(units, FEAT)),
+        raw=(2,),
+        scratch=[pltpu.VMEM((TOKENS, FEAT), F32), pltpu.VMEM((units, FEAT), BF16), pltpu.SemaphoreType.DMA((1,))],
     )
-
-    part = (keep + swap(send)).astype(BF16)
-    part = exchange(jnp.broadcast_to(part, (8,) + part.shape), ("zl", "y"))
-    part = jnp.sum(part.astype(F32), axis=0).astype(BF16)
-    part = exchange(jnp.broadcast_to(part, (4,) + part.shape), "zh")
-    own = lax.dynamic_slice_in_dim(residual, core * (TOKENS // 2), TOKENS // 2, 0)
-    own = (own + jnp.sum(part.astype(F32), axis=0)).astype(BF16)
-    theirs = swap(own)
-    first = core == 0
-    return jnp.concatenate([jnp.where(first, own, theirs), jnp.where(first, theirs, own)], axis=0)
+    (part,) = call(pair_body, [((8, TOKENS // 2, FEAT), BF16)], (keep, swap(send)))
+    (part,) = call(group_body, [((4, TOKENS // 2, FEAT), BF16)], (exchange(part, ("zl", "y")),))
+    (own,) = call(finish_body, [((TOKENS // 2, FEAT), BF16)], (exchange(part, "zh"), residual))
+    (out,) = call(assemble_body, [((TOKENS, FEAT), BF16)], (own, swap(own)), pinned=False)
+    return out
 
 
 def solution(mesh):

time: 97.6 us -> 91 us (0.932)
  blocking collectives: 58.3 us -> 68.2 us
  local copies, waits for them, and re-layouts: 9.38 us -> 0.02 us
  waiting for transfers between devices: 10.6 us -> 2.98 us
  Pallas kernels: 6.47 us -> 10.5 us
  starting transfers between devices: 11.3 us -> 8.89 us
    all_to_all x5 -> x6, blocking collectives: 58.3 us -> 68.2 us  [exchange(): return lax.all_to_all(v, axes, 0, 0, tiled=True)]
    unnamed x26 -> x10, local copies, waits for them, and re-layouts: 7.94 us -> 0.02 us
    all_to_all x1 -> x0, waiting for transfers between devices: 7.66 us -> none  [exchange(): return lax.all_to_all(v, axes, 0, 0, tiled=True)]
    pallas_call x5 -> x9, Pallas kernels: 6.47 us -> 10.5 us  [call(): run(*[pltpu.with_memory_space_constraint(a, space[k]) for a, k in zip(arg...]
    all_to_all x1 -> x0, starting transfers between devices: 3.36 us -> none  [exchange(): return lax.all_to_all(v, axes, 0, 0, tiled=True)]
    ppermute x3, starting transfers between devices: 7.9 us -> 8.89 us  [swap(): return lax.ppermute(v, 'core', [(0, 1), (1, 0)])]
  transfers between devices with their start and end apart: 4 -> 3, of which waited for: 4 -> 3; matrix products, arithmetic and copies ran while one was open for 0% -> 0% of each run, Pallas kernels for 0% -> 0%
where the time goes in v3:
time: 91 us; the launch traced here: 90.7 us
  blocking collectives  68.2 us (75%)
  Pallas kernels  10.5 us (12%)
  starting transfers between devices  8.89 us (10%)
  waiting for transfers between devices  2.98 us (3%)
    all_to_all x6, blocking collectives, exchange(): return lax.all_to_all(v, axes, 0, 0, tiled=True)  68.2 us
    pallas_call x9, Pallas kernels, call(): run(*[pltpu.with_memory_space_constraint(a, space[k]) for a, k in zip(arg...  10.5 us
    ppermute x3, starting transfers between devices, swap(): return lax.ppermute(v, 'core', [(0, 1), (1, 0)])  8.89 us
    ppermute x3, waiting for transfers between devices, swap(): return lax.ppermute(v, 'core', [(0, 1), (1, 0)])  2.98 us
  transfers between devices with their start and end apart: 3, of which 3 were waited for; matrix products, arithmetic and copies ran while one was open for 0% of the time, Pallas kernels for 0%

profile of v3, /device:TPU:1, one launch (start us, length us, event | category | flops | bytes accessed | tf_op | source)
XLA Modules:
  0.0 90.7 jit_solution(3735729656309901377)
XLA Ops:
  0.0 0.0 copy-start.2
  0.0 0.0 copy-start.3
  0.0 4.7 %shard_map.127 = bf16[8,32,256]{2,1,0:T(8,128)(2,1)S(1)} custom-call(s32[32]{0:T(128)} %len_ref.1, bf16[128,1536]{1,0:T(8,128)(2,1)} %tok_ref.1, f32[1536]{0:T(1024)} %gain_hbm.1, bf16[1536,640]{1,0:T(8,128)(2,1)} %w_hbm.1, bf16[1024,128]{1,0:T(8,128)(2,1)} %bitcast.14, bf16[1024,128]{1,0:T(8,128)(2,1)} %bitcast.15), custom_call_target="tpu_custom_call" | custom-call | flops 10000000 | bytes 1000000 | tf_op jit(solution)/shard_map/pallas_call | solution.py:59
  4.8 11.0 %all_to_all.30.in_ref = bf16[8,32,256]{2,1,0:T(8,128)(2,1)S(1)} all-to-all(bf16[8,32,256]{2,1,0:T(8,128)(2,1)S(1)} %shard_map.127), channel_id=1, replica_groups=mesh['zh'=4,'zl'=2,'y'=4,'core'=2,'tp'=4] {'y','core'}, dimensions={0} | all-to-all | bytes 262144 | tf_op jit(solution)/shard_map/all_to_all | solution.py:371
  15.8 0.3 shard_map.128
  16.2 15.8 %all_to_all.31.in_ref = bf16[8,32,256]{2,1,0:T(8,128)(2,1)S(1)} all-to-all(bf16[8,32,256]{2,1,0:T(8,128)(2,1)S(1)} %shard_map.128), channel_id=1, replica_groups=mesh['zh'=4,'zl'=2,'y'=4,'core'=2,'tp'=4] {'zh','zl'}, dimensions={0} | all-to-all | bytes 262144 | tf_op jit(solution)/shard_map/all_to_all | solution.py:371
  32.0 0.3 shard_map.129
  32.4 12.2 %all_to_all.32.mine_ref = bf16[16,32,256]{2,1,0:T(8,128)(2,1)S(1)} all-to-all(bf16[16,32,256]{2,1,0:T(8,128)(2,1)S(1)} %shard_map.129), channel_id=1, replica_groups=mesh['zh'=4,'zl'=2,'y'=4,'core'=2,'tp'=4] {'y','tp'}, dimensions={0} | all-to-all | bytes 524288 | tf_op jit(solution)/shard_map/all_to_all | solution.py:371
  44.6 3.7 %collective-permute-start = (bf16[16,32,256]{2,1,0:T(8,128)(2,1)S(1)}, bf16[16,32,256]{2,1,0:T(8,128)(2,1)S(1)}, u32[]{:S(2)}, u32[]{:S(2)}) collective-permute-start(bf16[16,32,256]{2,1,0:T(8,128)(2,1)S(1)} %all_to_all.32.mine_ref), channel_id=1, source_target_pairs={{0,4},{4,0},{1,5},{5,1},{2,6},{6,2},{3,7},{7,3},{8,12},{12,8},{9,1... | collective-permute-start | bytes 786440 | tf_op jit(solution)/shard_map/ppermute | solution.py:367
  48.2 0.0 copy-done.4
  48.2 1.2 %collective-permute-done.other_ref = bf16[16,32,256]{2,1,0:T(8,128)(2,1)S(1)} collective-permute-done((bf16[16,32,256]{2,1,0:T(8,128)(2,1)S(1)}, bf16[16,32,256]{2,1,0:T(8,128)(2,1)S(1)}, u32[]{:S(2)}, u32[]{:S(2)}) %collective-permute-start) | collective-permute-done | bytes 262176 | tf_op jit(solution)/shard_map/ppermute | solution.py:367
  49.4 0.0 copy-done
  49.4 0.0 copy-done.2
  49.4 2.6 %shard_map.130 = (f32[128,384]{1,0:T(8,128)S(1)}, bf16[4,128,256]{2,1,0:T(8,128)(2,1)S(1)}) custom-call(bf16[16,32,256]{2,1,0:T(8,128)(2,1)S(1)} %all_to_all.32.mine_ref, bf16[16,32,256]{2,1,0:T(8,128)(2,1)S(1)} %collective-permute-done.other_ref, bf16[128,1536]{1,0:T(8,128)(2,1)S(1)} %copy-done, bf16[1536,384]{1,0:T(8,128)(2,1)S(1)} %copy-done.1, ...), custom_call_target="tpu_custom_call" | custom-call | flops 10000000 | bytes 1000000 | tf_op jit(solution)/shard_map/pallas_call | solution.py:59
  52.0 8.8 %all_to_all.33.in_ref = bf16[4,128,256]{2,1,0:T(8,128)(2,1)S(1)} all-to-all(bf16[4,128,256]{2,1,0:T(8,128)(2,1)S(1)} %get-tuple-element.9), channel_id=1, replica_groups=mesh['zh'=4,'zl'=2,'y'=4,'core'=2,'tp'=4] {'tp'}, dimensions={0} | all-to-all | bytes 524288 | tf_op jit(solution)/shard_map/all_to_all | solution.py:371
  60.8 1.7 %shard_map.131 = (f32[64,384]{1,0:T(8,128)S(1)}, f32[64,384]{1,0:T(8,128)S(1)}) custom-call(bf16[4,128,256]{2,1,0:T(8,128)(2,1)S(1)} %all_to_all.33.in_ref, s32[8,128]{1,0:T(8,128)S(1)} %bitcast.13, bf16[320,384]{1,0:T(8,128)(2,1)} %bitcast.18), custom_call_target="tpu_custom_call" | custom-call | flops 10000000 | bytes 1000000 | tf_op jit(solution)/shard_map/pallas_call | solution.py:59
  62.6 1.3 %collective-permute-start.1 = (f32[64,384]{1,0:T(8,128)S(1)}, f32[64,384]{1,0:T(8,128)S(1)}, u32[]{:S(2)}, u32[]{:S(2)}) collective-permute-start(f32[64,384]{1,0:T(8,128)S(1)} %get-tuple-element.11), channel_id=1, source_target_pairs={{0,4},{4,0},{1,5},{5,1},{2,6},{6,2},{3,7},{7,3},{8,12},{12,8},{9,1... | collective-permute-start | bytes 294920 | tf_op jit(solution)/shard_map/ppermute | solution.py:367
  63.9 0.9 %collective-permute-done.1.got_ref = f32[64,384]{1,0:T(8,128)S(1)} collective-permute-done((f32[64,384]{1,0:T(8,128)S(1)}, f32[64,384]{1,0:T(8,128)S(1)}, u32[]{:S(2)}, u32[]{:S(2)}) %collective-permute-start.1) | collective-permute-done | bytes 98336 | tf_op jit(solution)/shard_map/ppermute | solution.py:367
  64.8 10.3 %all_to_all.34.in_ref = bf16[8,64,384]{2,1,0:T(8,128)(2,1)S(1)} all-to-all(bf16[8,64,384]{2,1,0:T(8,128)(2,1)S(1)} %shard_map.132), channel_id=1, replica_groups=mesh['zh'=4,'zl'=2,'y'=4,'core'=2,'tp'=4] {'zl','y'}, dimensions={0} | all-to-all | bytes 786432 | tf_op jit(solution)/shard_map/all_to_all | solution.py:371
  75.1 0.1 shard_map.133
  75.2 10.0 %all_to_all.35.in_ref = bf16[4,64,384]{2,1,0:T(8,128)(2,1)S(1)} all-to-all(bf16[4,64,384]{2,1,0:T(8,128)(2,1)S(1)} %shard_map.133), channel_id=1, replica_groups=mesh['zh'=4,'zl'=2,'y'=4,'core'=2,'tp'=4] {'zh'}, dimensions={0} | all-to-all | bytes 393216 | tf_op jit(solution)/shard_map/all_to_all | solution.py:371
  85.2 3.9 %collective-permute-start.2 = (bf16[64,384]{1,0:T(8,128)(2,1)S(1)}, bf16[64,384]{1,0:T(8,128)(2,1)S(1)}, u32[]{:S(2)}, u32[]{:S(2)}) collective-permute-start(bf16[64,384]{1,0:T(8,128)(2,1)S(1)} %shard_map.134.own_ref), channel_id=1, source_target_pairs={{0,4},{4,0},{1,5},{5,1},{2,6},{6,2},{3,7},{7,3},{8,12},{12,8},{9,1... | collective-permute-start | bytes 147464 | tf_op jit(solution)/shard_map/ppermute | solution.py:367
  89.1 0.9 collective-permute-done.2.other_ref
  90.0 0.7 shard_map.135
  (8 shorter events, 0.1 us)
Async XLA Ops:
  0.0 48.2 %copy-start.4 = (f32[384]{0:T(512)S(1)}, f32[384]{0:T(512)}, u32[]{:S(2)}) copy-start(f32[384]{0:T(512)} %param.17) | copy-start | bytes 4612
  0.0 49.4 %copy-start = (bf16[128,1536]{1,0:T(8,128)(2,1)S(1)}, bf16[128,1536]{1,0:T(8,128)(2,1)}, u32[]{:S(2)}) copy-start(bf16[128,1536]{1,0:T(8,128)(2,1)} %tok_ref.1) | copy-start | bytes 1179652
  0.0 49.4 %copy-start.1 = (bf16[1536,384]{1,0:T(8,128)(2,1)S(1)}, bf16[1536,384]{1,0:T(8,128)(2,1)}, u32[]{:S(2)}) copy-start(bf16[1536,384]{1,0:T(8,128)(2,1)} %w_ref.1) | copy-start | bytes 3538948
  0.0 49.4 %copy-start.2 = (bf16[384,40]{0,1:T(8,128)(2,1)S(1)}, bf16[384,40]{0,1:T(8,128)(2,1)}, u32[]{:S(2)}) copy-start(bf16[384,40]{0,1:T(8,128)(2,1)} %param.18) | copy-start | bytes 92164
  0.0 49.4 %copy-start.3 = (s32[128,8]{0,1:T(8,128)S(1)}, s32[128,8]{0,1:T(8,128)}, u32[]{:S(2)}) copy-start(s32[128,8]{0,1:T(8,128)} %param.25) | copy-start | bytes 12292
  44.6 4.8 %collective-permute-start = (bf16[16,32,256]{2,1,0:T(8,128)(2,1)S(1)}, bf16[16,32,256]{2,1,0:T(8,128)(2,1)S(1)}, u32[]{:S(2)}, u32[]{:S(2)}) collective-permute-start(bf16[16,32,256]{2,1,0:T(8,128)(2,1)S(1)} %all_to_all.32.mine_ref), channel_id=1, source_target_pairs={{0,4},{4,0},{1,5},{5,1},{2,6},{6,2},{3,7},{7,3},{8,12},{12,8},{9,1... | collective-permute-start | bytes 786440 | tf_op jit(solution)/shard_map/ppermute | solution.py:367
  62.6 2.2 %collective-permute-start.1 = (f32[64,384]{1,0:T(8,128)S(1)}, f32[64,384]{1,0:T(8,128)S(1)}, u32[]{:S(2)}, u32[]{:S(2)}) collective-permute-start(f32[64,384]{1,0:T(8,128)S(1)} %get-tuple-element.11), channel_id=1, source_target_pairs={{0,4},{4,0},{1,5},{5,1},{2,6},{6,2},{3,7},{7,3},{8,12},{12,8},{9,1... | collective-permute-start | bytes 294920 | tf_op jit(solution)/shard_map/ppermute | solution.py:367
  85.2 4.8 %collective-permute-start.2 = (bf16[64,384]{1,0:T(8,128)(2,1)S(1)}, bf16[64,384]{1,0:T(8,128)(2,1)S(1)}, u32[]{:S(2)}, u32[]{:S(2)}) collective-permute-start(bf16[64,384]{1,0:T(8,128)(2,1)S(1)} %shard_map.134.own_ref), channel_id=1, source_target_pairs={{0,4},{4,0},{1,5},{5,1},{2,6},{6,2},{3,7},{7,3},{8,12},{12,8},{9,1... | collective-permute-start | bytes 147464 | tf_op jit(solution)/shard_map/ppermute | solution.py:367

commit v4 on v3

--- a/solution.py
+++ b/solution.py
@@ -22,6 +22,7 @@
 FEAT = 384
 FF = 8
 CHUNKS = 4
+HALF = TOKENS // 2
 
 EPSILON = 1e-06
 ROPE_BASE = 10000.0
@@ -188,8 +189,9 @@
             e = [lse[g * 3 + q] for q in range(3)]
             stats = jnp.where(lane == 64, e[0], jnp.where(lane == 65, e[1], jnp.where(lane == 66, e[2], 0.0)))
             lo, hi = encode(jnp.where(low, a[0], a[1]), a[2], stats)
-            out_ref[grp * 2 + g, :, :128] = lo
-            out_ref[grp * 2 + g, :, 128:] = hi
+            for c in range(2):
+                out_ref[grp * 2 + c, :, 256 * g : 256 * g + 128] = lo[16 * c : 16 * c + 16]
+                out_ref[grp * 2 + c, :, 256 * g + 128 : 256 * g + 256] = hi[16 * c : 16 * c + 16]
 
 
 def merge(parts):
@@ -224,19 +226,25 @@
 
 
 def merge_y_body(in_ref, out_ref):
-    lo, hi = encode(*merge([decode(in_ref[i]) for i in range(8)]))
-    for i in range(8):
-        out_ref[i, :, :128] = lo
-        out_ref[i, :, 128:] = hi
+    for g in range(2):
+        at = slice(256 * g, 256 * g + 256)
+        lo, hi = encode(*merge([decode(in_ref[i, :, at]) for i in range(8)]))
+        for i in range(8):
+            out_ref[i, :, 256 * g : 256 * g + 128] = lo
+            out_ref[i, :, 256 * g + 128 : 256 * g + 256] = hi
 
 
 def merge_z_body(in_ref, out_ref):
-    lo, hi, _ = merge([decode(in_ref[i]) for i in range(8)])
-    lo = lo.astype(BF16)
-    hi = hi.astype(BF16)
-    for i in range(16):
-        out_ref[i, :, :128] = lo
-        out_ref[i, :, 128:] = hi
+    heads = []
+    for g in range(2):
+        at = slice(256 * g, 256 * g + 256)
+        heads.append(merge([decode(in_ref[i, :, at]) for i in range(8)]))
+    low = iota((16, 128), 1) < 64
+    last = jnp.where(low, heads[0][1], pltpu.roll(heads[1][1], 64, 1))
+    for j, v in enumerate((heads[0][0], heads[1][0], last)):
+        v = v.astype(BF16)
+        for i in range(16):
+            out_ref[i, :, 128 * j : 128 * j + 128] = v
 
 
 def split3(v):
@@ -246,103 +254,118 @@
     return a, b, (r - b.astype(F32)).astype(BF16)
 
 
+def own_rows(v, core):
+    v = v.reshape(4, 32, v.shape[-1])
+    return jnp.where(core == 0, v[:, :16], v[:, 16:]).reshape(HALF, v.shape[-1])
+
+
 def project_body(
     mine_ref,
-    other_ref,
+    w_ref,
     tok_ref,
-    w_ref,
-    gain_ref,
     router_ref,
-    gate_hbm,
-    up_hbm,
     routes_ref,
+    gain_hbm,
+    gate0_hbm,
+    up0_hbm,
+    gate1_hbm,
+    up1_hbm,
     res_ref,
     out_ref,
-    gate_ref,
-    up_ref,
+    gate0_ref,
+    up0_ref,
+    gate1_ref,
+    up1_ref,
+    gain_ref,
     sems,
 ):
-    copies = started([(gate_hbm, gate_ref), (up_hbm, up_ref)], sems)
     core = lax.axis_index("core")
     tp = lax.axis_index("tp")
-    acc = tok_ref[:, pl.ds(pl.multiple_of(tp * FEAT, 128), FEAT)].astype(F32)
-    for ref, c in ((mine_ref, core), (other_ref, 1 - core)):
-        for x in range(4):
-            a = jnp.concatenate([ref[y * 4 + x] for y in range(4)], axis=0)[:, :192]
-            at = pl.multiple_of((2 * x + c) * 192, 64)
-            acc = acc + dot(a, w_ref[pl.ds(at, 192), :])
+    pairs = [(gate0_hbm, gate0_ref), (up0_hbm, up0_ref), (gate1_hbm, gate1_ref), (up1_hbm, up1_ref)]
+    pairs.append((gain_hbm, gain_ref))
+    copies = started(pairs, sems)
+    acc = jnp.zeros((HALF, FEAT), F32)
+    for x in range(4):
+        a = jnp.concatenate([mine_ref[y * 4 + x] for y in range(4)], axis=0)
+        spans = [(0, 128), (192, 320), (128, 192), (320, 384)]
+        w = jnp.concatenate([w_ref[384 * x + i : 384 * x + j, :] for i, j in spans], axis=0)
+        acc = acc + dot(a, w)
+    own = own_rows(tok_ref[:, pl.ds(pl.multiple_of(tp * FEAT, 128), FEAT)].astype(F32), core)
+    acc = acc + own
     res_ref[...] = acc
-    gained = acc * gain_ref[...]
+    copies[4].wait()
+    gained = acc * gain_ref[...].reshape(1, FEAT)
     squares = jnp.sum(acc * acc, axis=-1, keepdims=True)
     router = router_ref[...]
     g0, g1, g2 = split3(gained)
     logits = dot_t(g0, router) + dot_t(g1, router) + dot_t(g2, router)
-    for c in copies:
-        c.wait()
-    both = jnp.concatenate([dot_t(g0, gate_ref[...]), dot_t(g0, up_ref[...])], axis=1)
-    routes = routes_ref[...].T
-    expert = (iota((TOKENS, 640), 1) % 320) // FF
-    elane = iota((TOKENS, EXPERTS), 1)
-    lane = iota((TOKENS, 128), 1)
+    routes = own_rows(routes_ref[...].T, core)
+    expert = (iota((HALF, 640), 1) % 320) // FF
+    elane = iota((HALF, EXPERTS), 1)
+    lane = iota((HALF, 128), 1)
     frow = iota((640, 128), 0)
     fcol = iota((640, 128), 1)
-    fold = (frow % FF == fcol % FF) & (frow // 320 == fcol // 64)
-    picks = jnp.zeros((TOKENS, 128), F32)
+    fold = ((frow % FF == fcol % 64) & (frow // 320 == fcol // 64)).astype(BF16)
     stats = jnp.where(lane == TOP, squares, 0.0)
     for k in range(TOP):
-        r = routes[:, k : k + 1]
-        chosen = jnp.sum(jnp.where(elane == r, logits, 0.0), axis=-1, keepdims=True)
+        chosen = jnp.sum(jnp.where(elane == routes[:, k : k + 1], logits, 0.0), axis=-1, keepdims=True)
         stats = jnp.where(lane == k, chosen, stats)
-        f = (fold & ((fcol % 64) // FF == k)).astype(BF16)
-        picks = picks + dot(jnp.where(expert == r, both, 0.0).astype(BF16), f)
+    for c in copies[:4]:
+        c.wait()
+    both = [
+        jnp.concatenate([dot_t(g0, gate0_ref[...]), dot_t(g0, up0_ref[...])], axis=1),
+        jnp.concatenate([dot_t(g0, gate1_ref[...]), dot_t(g0, up1_ref[...])], axis=1),
+    ]
+    chosen = [expert == routes[:, k : k + 1] for k in range(TOP)]
+    picks = []
+    for v in both:
+        v = jnp.concatenate([jnp.where(m, v, 0.0).astype(BF16) for m in chosen], axis=0)
+        v = dot(v, fold).reshape(TOP, HALF, 128)
+        picks.append(sum(v[k] if k == 0 else pltpu.roll(v[k], FF * k, 1) for k in range(TOP)))
     a, b, c = (v.astype(F32) for v in split3(stats))
     tail = (a + pltpu.roll(b, 16, 1) + pltpu.roll(c, 32, 1)).astype(BF16)
-    picks = picks.astype(BF16)
     for i in range(4):
-        out_ref[i, :, :128] = picks
-        out_ref[i, :, 128:] = tail
-
-
-def expert_body(in_ref, routes_ref, down_hbm, keep_ref, send_ref, part_ref, down_ref, sems):
-    copies = started([(down_hbm, down_ref)], sems)
+        out_ref[i, :, :128] = picks[0].astype(BF16)
+        out_ref[i, :, 128:256] = picks[1].astype(BF16)
+        out_ref[i, :, 256:] = tail
+
+
+def expert_body(in_ref, routes_ref, down0_hbm, down1_hbm, out_ref, down0_ref, down1_ref, sems):
     core = lax.axis_index("core")
-    lane = iota((TOKENS, 128), 1)
-    picks = sum(in_ref[i, :, :128].astype(F32) for i in range(4))
-    tail = sum(in_ref[i, :, 128:].astype(F32) for i in range(4))
+    copies = started([(down0_hbm, down0_ref), (down1_hbm, down1_ref)], sems)
+    lane = iota((HALF, 128), 1)
+    tail = sum(in_ref[i, :, 256:].astype(F32) for i in range(4))
     stats = tail + pltpu.roll(tail, 112, 1) + pltpu.roll(tail, 96, 1)
     scale = lax.rsqrt(stats[:, TOP : TOP + 1] / D + EPSILON)
     logits = jnp.where(lane < TOP, stats * scale, FLOOR_SCORE)
     weights = jnp.exp(logits - jnp.max(logits, axis=-1, keepdims=True))
     prob = weights / jnp.sum(weights, axis=-1, keepdims=True)
-    gate = picks * scale
-    up = pltpu.roll(gate, 64, 1)
-    activated = (gate / (1.0 + jnp.exp(-gate)) * up).astype(BF16).astype(F32)
-    wide = jnp.zeros((TOKENS, 128), F32)
+    wide = jnp.zeros((HALF, 128), F32)
     for k in range(TOP):
         wide = jnp.where(lane // FF == k, prob[:, k : k + 1], wide)
-    scaled = jnp.where(lane < 64, wide * activated, 0.0).astype(BF16)
     erow = iota((128, 1024), 0)
     ecol = iota((128, 1024), 1)
     spread_to = ((erow % FF == ecol % FF) & (erow // FF == ecol // 128)).astype(BF16)
-    tiled = dot(scaled, spread_to)
-    routes = routes_ref[...].T
-    spread = []
-    for i in range(3):
-        s = jnp.zeros((TOKENS, 128), F32)
-        for k in range(TOP):
-            s = jnp.where(lane // FF + 16 * i == routes[:, k : k + 1], tiled[:, 128 * k : 128 * k + 128], s)
-        spread.append(s)
-    spread = jnp.concatenate(spread, axis=1)[:, :320].astype(BF16)
-    copies[0].wait()
-    part_ref[...] = dot(spread, down_ref[...])
-    keep_ref[...] = part_ref[pl.ds(pl.multiple_of(core * 64, 64), 64), :]
-    send_ref[...] = part_ref[pl.ds(pl.multiple_of((1 - core) * 64, 64), 64), :]
-
-
-def pair_body(keep_ref, got_ref, out_ref):
-    v = (keep_ref[...] + got_ref[...]).astype(BF16)
+    tiled = []
+    for j in range(2):
+        gate = scale * sum(in_ref[i, :, 128 * j : 128 * j + 128].astype(F32) for i in range(4))
+        up = pltpu.roll(gate, 64, 1)
+        activated = (gate / (1.0 + jnp.exp(-gate)) * up).astype(BF16).astype(F32)
+        tiled.append(dot(jnp.where(lane < 64, wide * activated, 0.0).astype(BF16), spread_to))
+    routes = own_rows(routes_ref[...].T, core)
+    part = jnp.zeros((HALF, FEAT), F32)
+    for t, down_ref, copy in zip(tiled, (down0_ref, down1_ref), copies):
+        spread = []
+        for i in range(3):
+            s = jnp.zeros((HALF, 128), F32)
+            for k in range(TOP):
+                s = jnp.where(lane // FF + 16 * i == routes[:, k : k + 1], t[:, 128 * k : 128 * k + 128], s)
+            spread.append(s)
+        spread = jnp.concatenate(spread, axis=1)[:, :320].astype(BF16)
+        copy.wait()
+        part = part + dot(spread, down_ref[...])
     for i in range(8):
-        out_ref[i] = v
+        out_ref[i] = part.astype(BF16)
 
 
 def group_body(in_ref, out_ref):
@@ -352,15 +375,15 @@
 
 
 def finish_body(in_ref, res_ref, out_ref):
-    core = lax.axis_index("core")
-    own = res_ref[pl.ds(pl.multiple_of(core * 64, 64), 64), :]
-    out_ref[...] = (own + sum(in_ref[i].astype(F32) for i in range(4))).astype(BF16)
+    out_ref[...] = (res_ref[...] + sum(in_ref[i].astype(F32) for i in range(4))).astype(BF16)
 
 
 def assemble_body(own_ref, other_ref, out_ref):
     core = lax.axis_index("core")
-    out_ref[pl.ds(pl.multiple_of(core * 64, 64), 64), :] = own_ref[...]
-    out_ref[pl.ds(pl.multiple_of((1 - core) * 64, 64), 64), :] = other_ref[...]
+    for y in range(4):
+        rows = slice(16 * y, 16 * y + 16)
+        out_ref[pl.ds(pl.multiple_of(y * 32 + core * 16, 16), 16), :] = own_ref[rows]
+        out_ref[pl.ds(pl.multiple_of(y * 32 + (1 - core) * 16, 16), 16), :] = other_ref[rows]
 
 
 def swap(v):
@@ -388,9 +411,13 @@
 ):
     z = ("zh", "zl")
     units = EXPERTS * FF
+    gate = expert_gate.transpose(0, 2, 1).reshape(units, FEAT)
+    up = expert_up.transpose(0, 2, 1).reshape(units, FEAT)
+    down = expert_down.reshape(units, FEAT)
+    gate_there, up_there, down_there = swap(gate), swap(up), swap(down)
     (packed,) = call(
         attend_body,
-        [((8, 32, 256), BF16)],
+        [((8, 16, 512), BF16)],
         (
             lengths,
             tokens,
@@ -410,39 +437,36 @@
             pltpu.SemaphoreType.DMA((4 + CHUNKS,)),
         ],
     )
-    (packed,) = call(merge_y_body, [((8, 32, 256), BF16)], (exchange(packed, ("y", "core")),))
-    (packed,) = call(merge_z_body, [((16, 32, 256), BF16)], (exchange(packed, z),))
-    mine = exchange(packed, ("y", "tp"))
-    other = swap(mine)
-
+    packed, gate_there, up_there, down_there = lax.optimization_barrier((packed, gate_there, up_there, down_there))
+    (packed,) = call(merge_y_body, [((8, 16, 512), BF16)], (exchange(packed, ("y", "core")),))
+    (packed,) = call(merge_z_body, [((16, 16, 384), BF16)], (exchange(packed, z),))
     residual, picked = call(
         project_body,
-        [((TOKENS, FEAT), F32), ((4, TOKENS, 256), BF16)],
+        [((HALF, FEAT), F32), ((4, HALF, 384), BF16)],
         (
-            mine,
-            other,
+            exchange(packed, ("y", "tp")),
+            out_weight,
             tokens,
-            out_weight,
-            moe_gain.reshape(1, FEAT),
             router_weight.T,
-            expert_gate.transpose(0, 2, 1).reshape(units, FEAT),
-            expert_up.transpose(0, 2, 1).reshape(units, FEAT),
             routes.T,
+            moe_gain,
+            gate,
+            up,
+            gate_there,
+            up_there,
         ),
-        raw=(6, 7),
+        raw=(5, 6, 7, 8, 9),
+        scratch=[pltpu.VMEM((units, FEAT), BF16)] * 4 + [pltpu.VMEM((FEAT,), F32), pltpu.SemaphoreType.DMA((5,))],
+    )
+    (part,) = call(
+        expert_body,
+        [((8, HALF, FEAT), BF16)],
+        (exchange(picked, "tp"), routes.T, down, down_there),
+        raw=(2, 3),
         scratch=[pltpu.VMEM((units, FEAT), BF16)] * 2 + [pltpu.SemaphoreType.DMA((2,))],
     )
-    half = ((TOKENS // 2, FEAT), F32)
-    keep, send = call(
-        expert_body,
-        [half, half],
-        (exchange(picked, "tp"), routes.T, expert_down.reshape(units, FEAT)),
-        raw=(2,),
-        scratch=[pltpu.VMEM((TOKENS, FEAT), F32), pltpu.VMEM((units, FEAT), BF16), pltpu.SemaphoreType.DMA((1,))],
-    )
-    (part,) = call(pair_body, [((8, TOKENS // 2, FEAT), BF16)], (keep, swap(send)))
-    (part,) = call(group_body, [((4, TOKENS // 2, FEAT), BF16)], (exchange(part, ("zl", "y")),))
-    (own,) = call(finish_body, [((TOKENS // 2, FEAT), BF16)], (exchange(part, "zh"), residual))
+    (part,) = call(group_body, [((4, HALF, FEAT), BF16)], (exchange(part, ("zl", "y")),))
+    (own,) = call(finish_body, [((HALF, FEAT), BF16)], (exchange(part, "zh"), residual))
     (out,) = call(assemble_body, [((TOKENS, FEAT), BF16)], (own, swap(own)), pinned=False)
     return out
 

time: 91 us -> 86.4 us (0.949)
  blocking collectives: 68.2 us -> 62.5 us
  starting transfers between devices: 8.89 us -> 11.9 us
  waiting for transfers between devices: 2.98 us -> 0.89 us
    all_to_all x6, blocking collectives: 68.2 us -> 62.5 us  [exchange(): return lax.all_to_all(v, axes, 0, 0, tiled=True)]
    ppermute x3 -> x4, starting transfers between devices: 8.89 us -> 11.9 us  [swap(): return lax.ppermute(v, 'core', [(0, 1), (1, 0)])]
    ppermute x3 -> x4, waiting for transfers between devices: 2.98 us -> 0.89 us  [swap(): return lax.ppermute(v, 'core', [(0, 1), (1, 0)])]
    pallas_call x9 -> x8, Pallas kernels: 10.5 us -> 10.5 us  [call(): run(*[pltpu.with_memory_space_constraint(a, space[k]) for a, k in zip(arg...]
  transfers between devices with their start and end apart: 3 -> 4, of which waited for: 3 -> 1; matrix products, arithmetic and copies ran while one was open for 0% -> 0% of each run, Pallas kernels for 0% -> 5%
where the time goes in v4:
time: 86.4 us; the launch traced here: 86.1 us
  blocking collectives  62.5 us (72%)
  starting transfers between devices  11.9 us (14%)
  Pallas kernels  10.5 us (12%)
  waiting for transfers between devices  0.89 us (1%)
    all_to_all x6, blocking collectives, exchange(): return lax.all_to_all(v, axes, 0, 0, tiled=True)  62.5 us
    ppermute x4, starting transfers between devices, swap(): return lax.ppermute(v, 'core', [(0, 1), (1, 0)])  11.9 us
    pallas_call x8, Pallas kernels, call(): run(*[pltpu.with_memory_space_constraint(a, space[k]) for a, k in zip(arg...  10.5 us
  transfers between devices with their start and end apart: 4, of which 1 were waited for; matrix products, arithmetic and copies ran while one was open for 0% of the time, Pallas kernels for 5%

profile of v4, /device:TPU:1, one launch (start us, length us, event | category | flops | bytes accessed | tf_op | source)
XLA Modules:
  0.0 86.1 jit_solution(2513481931030570313)
XLA Ops:
  0.0 3.2 %collective-permute-start = (bf16[320,384]{1,0:T(8,128)(2,1)}, bf16[320,384]{1,0:T(8,128)(2,1)S(1)}, u32[]{:S(2)}, u32[]{:S(2)}) collective-permute-start(bf16[320,384]{1,0:T(8,128)(2,1)} %bitcast.18), channel_id=1, source_target_pairs={{0,4},{4,0},{1,5},{5,1},{2,6},{6,2},{3,7},{7,3},{8,12},{12,8},{9,1... | collective-permute-start | bytes 737288 | tf_op jit(solution)/shard_map/ppermute | solution.py:390
  3.2 0.0 collective-permute-start.1
  3.2 0.5 collective-permute-start.2
  3.8 4.7 %shard_map.127 = bf16[8,16,512]{2,1,0:T(8,128)(2,1)S(1)} custom-call(s32[32]{0:T(128)} %len_ref.1, bf16[128,1536]{1,0:T(8,128)(2,1)} %tok_ref.1, f32[1536]{0:T(1024)} %gain_hbm.2, bf16[1536,640]{1,0:T(8,128)(2,1)} %w_hbm.1, bf16[1024,128]{1,0:T(8,128)(2,1)} %bitcast.14, bf16[1024,128]{1,0:T(8,128)(2,1)} %bitcast.15), custom_call_target="tpu_custom_call" | custom-call | flops 10000000 | bytes 1000000 | tf_op jit(solution)/shard_map/pallas_call | solution.py:60
  8.5 0.0 collective-permute-done.gate1_hbm
  8.5 0.0 copy-start.5
  8.5 0.0 collective-permute-done.1.up1_hbm
  8.5 0.0 copy-start.6
  8.5 0.0 collective-permute-done.2.down1_hbm
  8.6 7.9 %all_to_all.30.in_ref = bf16[8,16,512]{2,1,0:T(8,128)(2,1)S(1)} all-to-all(bf16[8,16,512]{2,1,0:T(8,128)(2,1)S(1)} %shard_map.127), channel_id=1, replica_groups=mesh['zh'=4,'zl'=2,'y'=4,'core'=2,'tp'=4] {'y','core'}, dimensions={0} | all-to-all | bytes 262144 | tf_op jit(solution)/shard_map/all_to_all | solution.py:394
  16.5 0.4 shard_map.128
  16.9 15.8 %all_to_all.31.in_ref = bf16[8,16,512]{2,1,0:T(8,128)(2,1)S(1)} all-to-all(bf16[8,16,512]{2,1,0:T(8,128)(2,1)S(1)} %shard_map.128), channel_id=1, replica_groups=mesh['zh'=4,'zl'=2,'y'=4,'core'=2,'tp'=4] {'zh','zl'}, dimensions={0} | all-to-all | bytes 262144 | tf_op jit(solution)/shard_map/all_to_all | solution.py:394
  32.7 0.4 shard_map.129
  33.1 11.7 %all_to_all.32.mine_ref = bf16[16,16,384]{2,1,0:T(8,128)(2,1)S(1)} all-to-all(bf16[16,16,384]{2,1,0:T(8,128)(2,1)S(1)} %shard_map.129), channel_id=1, replica_groups=mesh['zh'=4,'zl'=2,'y'=4,'core'=2,'tp'=4] {'y','tp'}, dimensions={0} | all-to-all | bytes 393216 | tf_op jit(solution)/shard_map/all_to_all | solution.py:394
  44.8 3.0 %shard_map.130 = (f32[64,384]{1,0:T(8,128)S(1)}, bf16[4,64,384]{2,1,0:T(8,128)(2,1)S(1)}) custom-call(bf16[16,16,384]{2,1,0:T(8,128)(2,1)S(1)} %all_to_all.32.mine_ref, bf16[1536,384]{1,0:T(8,128)(2,1)S(1)} %copy-done.1, bf16[128,1536]{1,0:T(8,128)(2,1)S(1)} %copy-done, bf16[40,384]{1,0:T(8,128)(2,1)S(1)} %bitcast.11, s32[8,128]{1,0:T(8,128)S(1)} %bitcast.12, ...), custom_call_target="tpu_custom_call" | custom-call | flops 10000000 | bytes 1000000 | tf_op jit(solution)/shard_map/pallas_call | solution.py:60
  47.8 0.0 copy-done.4
  47.8 7.5 %all_to_all.33.in_ref = bf16[4,64,384]{2,1,0:T(8,128)(2,1)S(1)} all-to-all(bf16[4,64,384]{2,1,0:T(8,128)(2,1)S(1)} %get-tuple-element.14), channel_id=1, replica_groups=mesh['zh'=4,'zl'=2,'y'=4,'core'=2,'tp'=4] {'tp'}, dimensions={0} | all-to-all | bytes 393216 | tf_op jit(solution)/shard_map/all_to_all | solution.py:394
  55.4 1.3 %shard_map.131 = bf16[8,64,384]{2,1,0:T(8,128)(2,1)S(1)} custom-call(bf16[4,64,384]{2,1,0:T(8,128)(2,1)S(1)} %all_to_all.33.in_ref, s32[8,128]{1,0:T(8,128)S(1)} %bitcast.13, bf16[320,384]{1,0:T(8,128)(2,1)} %bitcast.17, bf16[320,384]{1,0:T(8,128)(2,1)} %copy-done.4), custom_call_target="tpu_custom_call" | custom-call | flops 10000000 | bytes 1000000 | tf_op jit(solution)/shard_map/pallas_call | solution.py:60
  56.7 9.2 %all_to_all.34.in_ref = bf16[8,64,384]{2,1,0:T(8,128)(2,1)S(1)} all-to-all(bf16[8,64,384]{2,1,0:T(8,128)(2,1)S(1)} %shard_map.131), channel_id=1, replica_groups=mesh['zh'=4,'zl'=2,'y'=4,'core'=2,'tp'=4] {'zl','y'}, dimensions={0} | all-to-all | bytes 786432 | tf_op jit(solution)/shard_map/all_to_all | solution.py:394
  65.9 0.1 shard_map.132
  66.0 10.3 %all_to_all.35.in_ref = bf16[4,64,384]{2,1,0:T(8,128)(2,1)S(1)} all-to-all(bf16[4,64,384]{2,1,0:T(8,128)(2,1)S(1)} %shard_map.132), channel_id=1, replica_groups=mesh['zh'=4,'zl'=2,'y'=4,'core'=2,'tp'=4] {'zh'}, dimensions={0} | all-to-all | bytes 393216 | tf_op jit(solution)/shard_map/all_to_all | solution.py:394
  76.3 8.2 %collective-permute-start.3 = (bf16[64,384]{1,0:T(8,128)(2,1)S(1)}, bf16[64,384]{1,0:T(8,128)(2,1)S(1)}, u32[]{:S(2)}, u32[]{:S(2)}) collective-permute-start(bf16[64,384]{1,0:T(8,128)(2,1)S(1)} %shard_map.133.own_ref), channel_id=1, source_target_pairs={{0,4},{4,0},{1,5},{5,1},{2,6},{6,2},{3,7},{7,3},{8,12},{12,8},{9,1... | collective-permute-start | bytes 147464 | tf_op jit(solution)/shard_map/ppermute | solution.py:390
  84.5 0.9 %collective-permute-done.3.other_ref = bf16[64,384]{1,0:T(8,128)(2,1)S(1)} collective-permute-done((bf16[64,384]{1,0:T(8,128)(2,1)S(1)}, bf16[64,384]{1,0:T(8,128)(2,1)S(1)}, u32[]{:S(2)}, u32[]{:S(2)}) %collective-permute-start.3) | collective-permute-done | bytes 49184 | tf_op jit(solution)/shard_map/ppermute | solution.py:390
  85.4 0.7 shard_map.134
  (12 shorter events, 0.1 us)
Async XLA Ops:
  0.0 8.5 %collective-permute-start = (bf16[320,384]{1,0:T(8,128)(2,1)}, bf16[320,384]{1,0:T(8,128)(2,1)S(1)}, u32[]{:S(2)}, u32[]{:S(2)}) collective-permute-start(bf16[320,384]{1,0:T(8,128)(2,1)} %bitcast.18), channel_id=1, source_target_pairs={{0,4},{4,0},{1,5},{5,1},{2,6},{6,2},{3,7},{7,3},{8,12},{12,8},{9,1... | collective-permute-start | bytes 737288 | tf_op jit(solution)/shard_map/ppermute | solution.py:390
  3.2 5.3 %collective-permute-start.1 = (bf16[320,384]{1,0:T(8,128)(2,1)}, bf16[320,384]{1,0:T(8,128)(2,1)S(1)}, u32[]{:S(2)}, u32[]{:S(2)}) collective-permute-start(bf16[320,384]{1,0:T(8,128)(2,1)} %bitcast.20), channel_id=1, source_target_pairs={{0,4},{4,0},{1,5},{5,1},{2,6},{6,2},{3,7},{7,3},{8,12},{12,8},{9,1... | collective-permute-start | bytes 737288 | tf_op jit(solution)/shard_map/ppermute | solution.py:390
  3.2 5.3 %collective-permute-start.2 = (bf16[320,384]{1,0:T(8,128)(2,1)}, bf16[320,384]{1,0:T(8,128)(2,1)S(1)}, u32[]{:S(2)}, u32[]{:S(2)}) collective-permute-start(bf16[320,384]{1,0:T(8,128)(2,1)} %bitcast.16), channel_id=1, source_target_pairs={{0,4},{4,0},{1,5},{5,1},{2,6},{6,2},{3,7},{7,3},{8,12},{12,8},{9,1... | collective-permute-start | bytes 737288 | tf_op jit(solution)/shard_map/ppermute | solution.py:390
  3.8 41.0 %copy-start = (bf16[128,1536]{1,0:T(8,128)(2,1)S(1)}, bf16[128,1536]{1,0:T(8,128)(2,1)}, u32[]{:S(2)}) copy-start(bf16[128,1536]{1,0:T(8,128)(2,1)} %tok_ref.1) | copy-start | bytes 1179652
  3.8 41.1 %copy-start.1 = (bf16[1536,384]{1,0:T(8,128)(2,1)S(1)}, bf16[1536,384]{1,0:T(8,128)(2,1)}, u32[]{:S(2)}) copy-start(bf16[1536,384]{1,0:T(8,128)(2,1)} %w_ref.1) | copy-start | bytes 3538948
  3.8 41.1 %copy-start.2 = (bf16[384,40]{0,1:T(8,128)(2,1)S(1)}, bf16[384,40]{0,1:T(8,128)(2,1)}, u32[]{:S(2)}) copy-start(bf16[384,40]{0,1:T(8,128)(2,1)} %param.18) | copy-start | bytes 92164
  3.8 41.1 %copy-start.3 = (s32[128,8]{0,1:T(8,128)S(1)}, s32[128,8]{0,1:T(8,128)}, u32[]{:S(2)}) copy-start(s32[128,8]{0,1:T(8,128)} %param.25) | copy-start | bytes 12292
  8.5 36.3 %copy-start.5 = (bf16[320,384]{1,0:T(8,128)(2,1)}, bf16[320,384]{1,0:T(8,128)(2,1)S(1)}, u32[]{:S(2)}) copy-start(bf16[320,384]{1,0:T(8,128)(2,1)S(1)} %collective-permute-done.gate1_hbm) | copy-start | bytes 737284
  8.5 36.3 %copy-start.6 = (bf16[320,384]{1,0:T(8,128)(2,1)}, bf16[320,384]{1,0:T(8,128)(2,1)S(1)}, u32[]{:S(2)}) copy-start(bf16[320,384]{1,0:T(8,128)(2,1)S(1)} %collective-permute-done.1.up1_hbm) | copy-start | bytes 737284
  8.6 39.3 %copy-start.4 = (bf16[320,384]{1,0:T(8,128)(2,1)}, bf16[320,384]{1,0:T(8,128)(2,1)S(1)}, u32[]{:S(2)}) copy-start(bf16[320,384]{1,0:T(8,128)(2,1)S(1)} %collective-permute-done.2.down1_hbm) | copy-start | bytes 737284
  76.3 9.1 %collective-permute-start.3 = (bf16[64,384]{1,0:T(8,128)(2,1)S(1)}, bf16[64,384]{1,0:T(8,128)(2,1)S(1)}, u32[]{:S(2)}, u32[]{:S(2)}) collective-permute-start(bf16[64,384]{1,0:T(8,128)(2,1)S(1)} %shard_map.133.own_ref), channel_id=1, source_target_pairs={{0,4},{4,0},{1,5},{5,1},{2,6},{6,2},{3,7},{7,3},{8,12},{12,8},{9,1... | collective-permute-start | bytes 147464 | tf_op jit(solution)/shard_map/ppermute | solution.py:390

commit v5 on v4

--- a/solution.py
+++ b/solution.py
@@ -265,24 +265,21 @@
     tok_ref,
     router_ref,
     routes_ref,
+    gate1_ref,
+    up1_ref,
     gain_hbm,
     gate0_hbm,
     up0_hbm,
-    gate1_hbm,
-    up1_hbm,
     res_ref,
     out_ref,
     gate0_ref,
     up0_ref,
-    gate1_ref,
-    up1_ref,
     gain_ref,
     sems,
 ):
     core = lax.axis_index("core")
     tp = lax.axis_index("tp")
-    pairs = [(gate0_hbm, gate0_ref), (up0_hbm, up0_ref), (gate1_hbm, gate1_ref), (up1_hbm, up1_ref)]
-    pairs.append((gain_hbm, gain_ref))
+    pairs = [(gate0_hbm, gate0_ref), (up0_hbm, up0_ref), (gain_hbm, gain_ref)]
     copies = started(pairs, sems)
     acc = jnp.zeros((HALF, FEAT), F32)
     for x in range(4):
@@ -293,7 +290,7 @@
     own = own_rows(tok_ref[:, pl.ds(pl.multiple_of(tp * FEAT, 128), FEAT)].astype(F32), core)
     acc = acc + own
     res_ref[...] = acc
-    copies[4].wait()
+    copies[2].wait()
     gained = acc * gain_ref[...].reshape(1, FEAT)
     squares = jnp.sum(acc * acc, axis=-1, keepdims=True)
     router = router_ref[...]
@@ -310,7 +307,7 @@
     for k in range(TOP):
         chosen = jnp.sum(jnp.where(elane == routes[:, k : k + 1], logits, 0.0), axis=-1, keepdims=True)
         stats = jnp.where(lane == k, chosen, stats)
-    for c in copies[:4]:
+    for c in copies[:2]:
         c.wait()
     both = [
         jnp.concatenate([dot_t(g0, gate0_ref[...]), dot_t(g0, up0_ref[...])], axis=1),
@@ -330,9 +327,9 @@
         out_ref[i, :, 256:] = tail
 
 
-def expert_body(in_ref, routes_ref, down0_hbm, down1_hbm, out_ref, down0_ref, down1_ref, sems):
+def expert_body(in_ref, routes_ref, down1_ref, down0_hbm, out_ref, down0_ref, sems):
     core = lax.axis_index("core")
-    copies = started([(down0_hbm, down0_ref), (down1_hbm, down1_ref)], sems)
+    copies = started([(down0_hbm, down0_ref)], sems)
     lane = iota((HALF, 128), 1)
     tail = sum(in_ref[i, :, 256:].astype(F32) for i in range(4))
     stats = tail + pltpu.roll(tail, 112, 1) + pltpu.roll(tail, 96, 1)
@@ -354,7 +351,7 @@
         tiled.append(dot(jnp.where(lane < 64, wide * activated, 0.0).astype(BF16), spread_to))
     routes = own_rows(routes_ref[...].T, core)
     part = jnp.zeros((HALF, FEAT), F32)
-    for t, down_ref, copy in zip(tiled, (down0_ref, down1_ref), copies):
+    for t, down_ref in zip(tiled[::-1], (down1_ref, down0_ref)):
         spread = []
         for i in range(3):
             s = jnp.zeros((HALF, 128), F32)
@@ -362,7 +359,8 @@
                 s = jnp.where(lane // FF + 16 * i == routes[:, k : k + 1], t[:, 128 * k : 128 * k + 128], s)
             spread.append(s)
         spread = jnp.concatenate(spread, axis=1)[:, :320].astype(BF16)
-        copy.wait()
+        if down_ref is down0_ref:
+            copies[0].wait()
         part = part + dot(spread, down_ref[...])
     for i in range(8):
         out_ref[i] = part.astype(BF16)
@@ -449,21 +447,21 @@
             tokens,
             router_weight.T,
             routes.T,
+            gate_there,
+            up_there,
             moe_gain,
             gate,
             up,
-            gate_there,
-            up_there,
         ),
-        raw=(5, 6, 7, 8, 9),
-        scratch=[pltpu.VMEM((units, FEAT), BF16)] * 4 + [pltpu.VMEM((FEAT,), F32), pltpu.SemaphoreType.DMA((5,))],
+        raw=(7, 8, 9),
+        scratch=[pltpu.VMEM((units, FEAT), BF16)] * 2 + [pltpu.VMEM((FEAT,), F32), pltpu.SemaphoreType.DMA((3,))],
     )
     (part,) = call(
         expert_body,
         [((8, HALF, FEAT), BF16)],
-        (exchange(picked, "tp"), routes.T, down, down_there),
-        raw=(2, 3),
-        scratch=[pltpu.VMEM((units, FEAT), BF16)] * 2 + [pltpu.SemaphoreType.DMA((2,))],
+        (exchange(picked, "tp"), routes.T, down_there, down),
+        raw=(3,),
+        scratch=[pltpu.VMEM((units, FEAT), BF16), pltpu.SemaphoreType.DMA((1,))],
     )
     (part,) = call(group_body, [((4, HALF, FEAT), BF16)], (exchange(part, ("zl", "y")),))
     (own,) = call(finish_body, [((HALF, FEAT), BF16)], (exchange(part, "zh"), residual))

time: 86.4 us -> 86 us (level)
  transfers between devices with their start and end apart: 4 -> 4, of which waited for: 1 -> 1; matrix products, arithmetic and copies ran while one was open for 0% -> 0% of each run, Pallas kernels for 5% -> 6%
where the time goes in v5:
time: 86 us; the launch traced here: 85.7 us
  blocking collectives  62.5 us (73%)
  starting transfers between devices  11.9 us (14%)
  Pallas kernels  10.2 us (12%)
  waiting for transfers between devices  0.89 us (1%)
    all_to_all x6, blocking collectives, exchange(): return lax.all_to_all(v, axes, 0, 0, tiled=True)  62.5 us
    ppermute x4, starting transfers between devices, swap(): return lax.ppermute(v, 'core', [(0, 1), (1, 0)])  11.9 us
    pallas_call x8, Pallas kernels, call(): run(*[pltpu.with_memory_space_constraint(a, space[k]) for a, k in zip(arg...  10.2 us
  transfers between devices with their start and end apart: 4, of which 1 were waited for; matrix products, arithmetic and copies ran while one was open for 0% of the time, Pallas kernels for 6%

profile of v5, /device:TPU:1, one launch (start us, length us, event | category | flops | bytes accessed | tf_op | source)
XLA Modules:
  0.0 85.7 jit_solution(15020069566398207762)
XLA Ops:
  0.0 3.2 %collective-permute-start = (bf16[320,384]{1,0:T(8,128)(2,1)}, bf16[320,384]{1,0:T(8,128)(2,1)S(1)}, u32[]{:S(2)}, u32[]{:S(2)}) collective-permute-start(bf16[320,384]{1,0:T(8,128)(2,1)} %bitcast.18), channel_id=1, source_target_pairs={{0,4},{4,0},{1,5},{5,1},{2,6},{6,2},{3,7},{7,3},{8,12},{12,8},{9,1... | collective-permute-start | bytes 737288 | tf_op jit(solution)/shard_map/ppermute | solution.py:388
  3.2 0.0 collective-permute-start.1
  3.2 0.5 collective-permute-start.2
  3.8 4.7 %shard_map.127 = bf16[8,16,512]{2,1,0:T(8,128)(2,1)S(1)} custom-call(s32[32]{0:T(128)} %len_ref.1, bf16[128,1536]{1,0:T(8,128)(2,1)} %tok_ref.1, f32[1536]{0:T(1024)} %gain_hbm.2, bf16[1536,640]{1,0:T(8,128)(2,1)} %w_hbm.1, bf16[1024,128]{1,0:T(8,128)(2,1)} %bitcast.14, bf16[1024,128]{1,0:T(8,128)(2,1)} %bitcast.15), custom_call_target="tpu_custom_call" | custom-call | flops 10000000 | bytes 1000000 | tf_op jit(solution)/shard_map/pallas_call | solution.py:60
  8.5 0.0 collective-permute-done.gate1_ref
  8.5 0.0 collective-permute-done.1.up1_ref
  8.5 0.0 collective-permute-done.2.down1_ref
  8.5 7.9 %all_to_all.30.in_ref = bf16[8,16,512]{2,1,0:T(8,128)(2,1)S(1)} all-to-all(bf16[8,16,512]{2,1,0:T(8,128)(2,1)S(1)} %shard_map.127), channel_id=1, replica_groups=mesh['zh'=4,'zl'=2,'y'=4,'core'=2,'tp'=4] {'y','core'}, dimensions={0} | all-to-all | bytes 262144 | tf_op jit(solution)/shard_map/all_to_all | solution.py:392
  16.5 0.4 shard_map.128
  16.8 15.8 %all_to_all.31.in_ref = bf16[8,16,512]{2,1,0:T(8,128)(2,1)S(1)} all-to-all(bf16[8,16,512]{2,1,0:T(8,128)(2,1)S(1)} %shard_map.128), channel_id=1, replica_groups=mesh['zh'=4,'zl'=2,'y'=4,'core'=2,'tp'=4] {'zh','zl'}, dimensions={0} | all-to-all | bytes 262144 | tf_op jit(solution)/shard_map/all_to_all | solution.py:392
  32.7 0.4 shard_map.129
  33.0 11.7 %all_to_all.32.mine_ref = bf16[16,16,384]{2,1,0:T(8,128)(2,1)S(1)} all-to-all(bf16[16,16,384]{2,1,0:T(8,128)(2,1)S(1)} %shard_map.129), channel_id=1, replica_groups=mesh['zh'=4,'zl'=2,'y'=4,'core'=2,'tp'=4] {'y','tp'}, dimensions={0} | all-to-all | bytes 393216 | tf_op jit(solution)/shard_map/all_to_all | solution.py:392
  44.8 0.0 copy-done
  44.8 0.0 copy-done.1
  44.8 0.0 copy-done.2
  44.8 2.8 %shard_map.130 = (f32[64,384]{1,0:T(8,128)S(1)}, bf16[4,64,384]{2,1,0:T(8,128)(2,1)S(1)}) custom-call(bf16[16,16,384]{2,1,0:T(8,128)(2,1)S(1)} %all_to_all.32.mine_ref, bf16[1536,384]{1,0:T(8,128)(2,1)S(1)} %copy-done.1, bf16[128,1536]{1,0:T(8,128)(2,1)S(1)} %copy-done, bf16[40,384]{1,0:T(8,128)(2,1)S(1)} %bitcast.11, s32[8,128]{1,0:T(8,128)S(1)} %bitcast.12, ...), custom_call_target="tpu_custom_call" | custom-call | flops 10000000 | bytes 1000000 | tf_op jit(solution)/shard_map/pallas_call | solution.py:60
  47.6 7.5 %all_to_all.33.in_ref = bf16[4,64,384]{2,1,0:T(8,128)(2,1)S(1)} all-to-all(bf16[4,64,384]{2,1,0:T(8,128)(2,1)S(1)} %get-tuple-element.14), channel_id=1, replica_groups=mesh['zh'=4,'zl'=2,'y'=4,'core'=2,'tp'=4] {'tp'}, dimensions={0} | all-to-all | bytes 393216 | tf_op jit(solution)/shard_map/all_to_all | solution.py:392
  55.1 1.2 %shard_map.131 = bf16[8,64,384]{2,1,0:T(8,128)(2,1)S(1)} custom-call(bf16[4,64,384]{2,1,0:T(8,128)(2,1)S(1)} %all_to_all.33.in_ref, s32[8,128]{1,0:T(8,128)S(1)} %bitcast.13, bf16[320,384]{1,0:T(8,128)(2,1)S(1)} %collective-permute-done.2.down1_ref, bf16[320,384]{1,0:T(8,128)(2,1)} %bitcast.17), custom_call_target="tpu_custom_call" | custom-call | flops 10000000 | bytes 1000000 | tf_op jit(solution)/shard_map/pallas_call | solution.py:60
  56.3 9.2 %all_to_all.34.in_ref = bf16[8,64,384]{2,1,0:T(8,128)(2,1)S(1)} all-to-all(bf16[8,64,384]{2,1,0:T(8,128)(2,1)S(1)} %shard_map.131), channel_id=1, replica_groups=mesh['zh'=4,'zl'=2,'y'=4,'core'=2,'tp'=4] {'zl','y'}, dimensions={0} | all-to-all | bytes 786432 | tf_op jit(solution)/shard_map/all_to_all | solution.py:392
  65.5 0.1 shard_map.132
  65.6 10.3 %all_to_all.35.in_ref = bf16[4,64,384]{2,1,0:T(8,128)(2,1)S(1)} all-to-all(bf16[4,64,384]{2,1,0:T(8,128)(2,1)S(1)} %shard_map.132), channel_id=1, replica_groups=mesh['zh'=4,'zl'=2,'y'=4,'core'=2,'tp'=4] {'zh'}, dimensions={0} | all-to-all | bytes 393216 | tf_op jit(solution)/shard_map/all_to_all | solution.py:392
  75.9 8.2 %collective-permute-start.3 = (bf16[64,384]{1,0:T(8,128)(2,1)S(1)}, bf16[64,384]{1,0:T(8,128)(2,1)S(1)}, u32[]{:S(2)}, u32[]{:S(2)}) collective-permute-start(bf16[64,384]{1,0:T(8,128)(2,1)S(1)} %shard_map.133.own_ref), channel_id=1, source_target_pairs={{0,4},{4,0},{1,5},{5,1},{2,6},{6,2},{3,7},{7,3},{8,12},{12,8},{9,1... | collective-permute-start | bytes 147464 | tf_op jit(solution)/shard_map/ppermute | solution.py:388
  84.1 0.9 %collective-permute-done.3.other_ref = bf16[64,384]{1,0:T(8,128)(2,1)S(1)} collective-permute-done((bf16[64,384]{1,0:T(8,128)(2,1)S(1)}, bf16[64,384]{1,0:T(8,128)(2,1)S(1)}, u32[]{:S(2)}, u32[]{:S(2)}) %collective-permute-start.3) | collective-permute-done | bytes 49184 | tf_op jit(solution)/shard_map/ppermute | solution.py:388
  85.0 0.7 shard_map.134
  (6 shorter events, 0.0 us)
Async XLA Ops:
  0.0 8.5 %collective-permute-start = (bf16[320,384]{1,0:T(8,128)(2,1)}, bf16[320,384]{1,0:T(8,128)(2,1)S(1)}, u32[]{:S(2)}, u32[]{:S(2)}) collective-permute-start(bf16[320,384]{1,0:T(8,128)(2,1)} %bitcast.18), channel_id=1, source_target_pairs={{0,4},{4,0},{1,5},{5,1},{2,6},{6,2},{3,7},{7,3},{8,12},{12,8},{9,1... | collective-permute-start | bytes 737288 | tf_op jit(solution)/shard_map/ppermute | solution.py:388
  3.2 5.3 %collective-permute-start.1 = (bf16[320,384]{1,0:T(8,128)(2,1)}, bf16[320,384]{1,0:T(8,128)(2,1)S(1)}, u32[]{:S(2)}, u32[]{:S(2)}) collective-permute-start(bf16[320,384]{1,0:T(8,128)(2,1)} %bitcast.20), channel_id=1, source_target_pairs={{0,4},{4,0},{1,5},{5,1},{2,6},{6,2},{3,7},{7,3},{8,12},{12,8},{9,1... | collective-permute-start | bytes 737288 | tf_op jit(solution)/shard_map/ppermute | solution.py:388
  3.2 5.3 %collective-permute-start.2 = (bf16[320,384]{1,0:T(8,128)(2,1)}, bf16[320,384]{1,0:T(8,128)(2,1)S(1)}, u32[]{:S(2)}, u32[]{:S(2)}) collective-permute-start(bf16[320,384]{1,0:T(8,128)(2,1)} %bitcast.16), channel_id=1, source_target_pairs={{0,4},{4,0},{1,5},{5,1},{2,6},{6,2},{3,7},{7,3},{8,12},{12,8},{9,1... | collective-permute-start | bytes 737288 | tf_op jit(solution)/shard_map/ppermute | solution.py:388
  3.8 41.0 %copy-start = (bf16[128,1536]{1,0:T(8,128)(2,1)S(1)}, bf16[128,1536]{1,0:T(8,128)(2,1)}, u32[]{:S(2)}) copy-start(bf16[128,1536]{1,0:T(8,128)(2,1)} %tok_ref.1) | copy-start | bytes 1179652
  3.8 41.0 %copy-start.1 = (bf16[1536,384]{1,0:T(8,128)(2,1)S(1)}, bf16[1536,384]{1,0:T(8,128)(2,1)}, u32[]{:S(2)}) copy-start(bf16[1536,384]{1,0:T(8,128)(2,1)} %w_ref.1) | copy-start | bytes 3538948
  3.8 41.0 %copy-start.2 = (bf16[384,40]{0,1:T(8,128)(2,1)S(1)}, bf16[384,40]{0,1:T(8,128)(2,1)}, u32[]{:S(2)}) copy-start(bf16[384,40]{0,1:T(8,128)(2,1)} %param.18) | copy-start | bytes 92164
  3.8 41.0 %copy-start.3 = (s32[128,8]{0,1:T(8,128)S(1)}, s32[128,8]{0,1:T(8,128)}, u32[]{:S(2)}) copy-start(s32[128,8]{0,1:T(8,128)} %param.25) | copy-start | bytes 12292
  75.9 9.1 %collective-permute-start.3 = (bf16[64,384]{1,0:T(8,128)(2,1)S(1)}, bf16[64,384]{1,0:T(8,128)(2,1)S(1)}, u32[]{:S(2)}, u32[]{:S(2)}) collective-permute-start(bf16[64,384]{1,0:T(8,128)(2,1)S(1)} %shard_map.133.own_ref), channel_id=1, source_target_pairs={{0,4},{4,0},{1,5},{5,1},{2,6},{6,2},{3,7},{7,3},{8,12},{12,8},{9,1... | collective-permute-start | bytes 147464 | tf_op jit(solution)/shard_map/ppermute | solution.py:388

commit v6 on v5

--- a/solution.py
+++ b/solution.py
@@ -297,28 +297,32 @@
     g0, g1, g2 = split3(gained)
     logits = dot_t(g0, router) + dot_t(g1, router) + dot_t(g2, router)
     routes = own_rows(routes_ref[...].T, core)
-    expert = (iota((HALF, 640), 1) % 320) // FF
     elane = iota((HALF, EXPERTS), 1)
     lane = iota((HALF, 128), 1)
-    frow = iota((640, 128), 0)
-    fcol = iota((640, 128), 1)
-    fold = ((frow % FF == fcol % 64) & (frow // 320 == fcol // 64)).astype(BF16)
+    frow = iota((256, 128), 0)
+    fcol = iota((256, 128), 1)
+    fold = ((frow % FF == fcol % 64) & (frow // 128 == fcol // 64)).astype(BF16)
     stats = jnp.where(lane == TOP, squares, 0.0)
     for k in range(TOP):
         chosen = jnp.sum(jnp.where(elane == routes[:, k : k + 1], logits, 0.0), axis=-1, keepdims=True)
         stats = jnp.where(lane == k, chosen, stats)
-    for c in copies[:2]:
-        c.wait()
-    both = [
-        jnp.concatenate([dot_t(g0, gate0_ref[...]), dot_t(g0, up0_ref[...])], axis=1),
-        jnp.concatenate([dot_t(g0, gate1_ref[...]), dot_t(g0, up1_ref[...])], axis=1),
-    ]
-    chosen = [expert == routes[:, k : k + 1] for k in range(TOP)]
+    masks = [[lane // FF + 16 * i == routes[:, k : k + 1] for i in range(3)] for k in range(TOP)]
+    blank = jnp.zeros((HALF, 64), F32)
+
+    def picked(weight_ref):
+        v = jnp.concatenate([dot_t(g0, weight_ref[...]), blank], axis=1)
+        t = [v[:, 128 * i : 128 * i + 128] for i in range(3)]
+        rows = [jnp.where(m[0], t[0], jnp.where(m[1], t[1], jnp.where(m[2], t[2], 0.0))) for m in masks]
+        return jnp.concatenate([r.astype(BF16) for r in rows], axis=0)
+
     picks = []
-    for v in both:
-        v = jnp.concatenate([jnp.where(m, v, 0.0).astype(BF16) for m in chosen], axis=0)
+    for gate_ref, up_ref in ((gate1_ref, up1_ref), (gate0_ref, up0_ref)):
+        if gate_ref is gate0_ref:
+            for c in copies[:2]:
+                c.wait()
+        v = jnp.concatenate([picked(gate_ref), picked(up_ref)], axis=1)
         v = dot(v, fold).reshape(TOP, HALF, 128)
-        picks.append(sum(v[k] if k == 0 else pltpu.roll(v[k], FF * k, 1) for k in range(TOP)))
+        picks.insert(0, sum(v[k] if k == 0 else pltpu.roll(v[k], FF * k, 1) for k in range(TOP)))
     a, b, c = (v.astype(F32) for v in split3(stats))
     tail = (a + pltpu.roll(b, 16, 1) + pltpu.roll(c, 32, 1)).astype(BF16)
     for i in range(4):

time: 86 us -> 86 us (level)
  no operation moved by 1% of the time
where the time goes in v6:
time: 86 us; the launch traced here: 85.6 us
  blocking collectives  62.5 us (73%)
  starting transfers between devices  11.9 us (14%)
  Pallas kernels  10.1 us (12%)
  waiting for transfers between devices  0.89 us (1%)
    all_to_all x6, blocking collectives, exchange(): return lax.all_to_all(v, axes, 0, 0, tiled=True)  62.5 us
    ppermute x4, starting transfers between devices, swap(): return lax.ppermute(v, 'core', [(0, 1), (1, 0)])  11.9 us
    pallas_call x8, Pallas kernels, call(): run(*[pltpu.with_memory_space_constraint(a, space[k]) for a, k in zip(arg...  10.1 us
  transfers between devices with their start and end apart: 4, of which 1 were waited for; matrix products, arithmetic and copies ran while one was open for 0% of the time, Pallas kernels for 6%

profile of v6, /device:TPU:1, one launch (start us, length us, event | category | flops | bytes accessed | tf_op | source)
XLA Modules:
  0.0 85.6 jit_solution(50747612798506710)
XLA Ops:
  0.0 3.2 %collective-permute-start = (bf16[320,384]{1,0:T(8,128)(2,1)}, bf16[320,384]{1,0:T(8,128)(2,1)S(1)}, u32[]{:S(2)}, u32[]{:S(2)}) collective-permute-start(bf16[320,384]{1,0:T(8,128)(2,1)} %bitcast.18), channel_id=1, source_target_pairs={{0,4},{4,0},{1,5},{5,1},{2,6},{6,2},{3,7},{7,3},{8,12},{12,8},{9,1... | collective-permute-start | bytes 737288 | tf_op jit(solution)/shard_map/ppermute | solution.py:392
  3.2 0.0 collective-permute-start.1
  3.2 0.5 collective-permute-start.2
  3.8 4.7 %shard_map.127 = bf16[8,16,512]{2,1,0:T(8,128)(2,1)S(1)} custom-call(s32[32]{0:T(128)} %len_ref.1, bf16[128,1536]{1,0:T(8,128)(2,1)} %tok_ref.1, f32[1536]{0:T(1024)} %gain_hbm.2, bf16[1536,640]{1,0:T(8,128)(2,1)} %w_hbm.1, bf16[1024,128]{1,0:T(8,128)(2,1)} %bitcast.14, bf16[1024,128]{1,0:T(8,128)(2,1)} %bitcast.15), custom_call_target="tpu_custom_call" | custom-call | flops 10000000 | bytes 1000000 | tf_op jit(solution)/shard_map/pallas_call | solution.py:60
  8.5 0.0 collective-permute-done.gate1_ref
  8.5 0.0 collective-permute-done.1.up1_ref
  8.5 0.0 collective-permute-done.2.down1_ref
  8.5 7.9 %all_to_all.30.in_ref = bf16[8,16,512]{2,1,0:T(8,128)(2,1)S(1)} all-to-all(bf16[8,16,512]{2,1,0:T(8,128)(2,1)S(1)} %shard_map.127), channel_id=1, replica_groups=mesh['zh'=4,'zl'=2,'y'=4,'core'=2,'tp'=4] {'y','core'}, dimensions={0} | all-to-all | bytes 262144 | tf_op jit(solution)/shard_map/all_to_all | solution.py:396
  16.5 0.4 shard_map.128
  16.8 15.8 %all_to_all.31.in_ref = bf16[8,16,512]{2,1,0:T(8,128)(2,1)S(1)} all-to-all(bf16[8,16,512]{2,1,0:T(8,128)(2,1)S(1)} %shard_map.128), channel_id=1, replica_groups=mesh['zh'=4,'zl'=2,'y'=4,'core'=2,'tp'=4] {'zh','zl'}, dimensions={0} | all-to-all | bytes 262144 | tf_op jit(solution)/shard_map/all_to_all | solution.py:396
  32.7 0.4 shard_map.129
  33.0 11.7 %all_to_all.32.mine_ref = bf16[16,16,384]{2,1,0:T(8,128)(2,1)S(1)} all-to-all(bf16[16,16,384]{2,1,0:T(8,128)(2,1)S(1)} %shard_map.129), channel_id=1, replica_groups=mesh['zh'=4,'zl'=2,'y'=4,'core'=2,'tp'=4] {'y','tp'}, dimensions={0} | all-to-all | bytes 393216 | tf_op jit(solution)/shard_map/all_to_all | solution.py:396
  44.8 0.0 copy-done
  44.8 0.0 copy-done.1
  44.8 0.0 copy-done.2
  44.8 2.7 %shard_map.130 = (f32[64,384]{1,0:T(8,128)S(1)}, bf16[4,64,384]{2,1,0:T(8,128)(2,1)S(1)}) custom-call(bf16[16,16,384]{2,1,0:T(8,128)(2,1)S(1)} %all_to_all.32.mine_ref, bf16[1536,384]{1,0:T(8,128)(2,1)S(1)} %copy-done.1, bf16[128,1536]{1,0:T(8,128)(2,1)S(1)} %copy-done, bf16[40,384]{1,0:T(8,128)(2,1)S(1)} %bitcast.11, s32[8,128]{1,0:T(8,128)S(1)} %bitcast.12, ...), custom_call_target="tpu_custom_call" | custom-call | flops 10000000 | bytes 1000000 | tf_op jit(solution)/shard_map/pallas_call | solution.py:60
  47.5 7.5 %all_to_all.33.in_ref = bf16[4,64,384]{2,1,0:T(8,128)(2,1)S(1)} all-to-all(bf16[4,64,384]{2,1,0:T(8,128)(2,1)S(1)} %get-tuple-element.14), channel_id=1, replica_groups=mesh['zh'=4,'zl'=2,'y'=4,'core'=2,'tp'=4] {'tp'}, dimensions={0} | all-to-all | bytes 393216 | tf_op jit(solution)/shard_map/all_to_all | solution.py:396
  55.0 1.2 %shard_map.131 = bf16[8,64,384]{2,1,0:T(8,128)(2,1)S(1)} custom-call(bf16[4,64,384]{2,1,0:T(8,128)(2,1)S(1)} %all_to_all.33.in_ref, s32[8,128]{1,0:T(8,128)S(1)} %bitcast.13, bf16[320,384]{1,0:T(8,128)(2,1)S(1)} %collective-permute-done.2.down1_ref, bf16[320,384]{1,0:T(8,128)(2,1)} %bitcast.17), custom_call_target="tpu_custom_call" | custom-call | flops 10000000 | bytes 1000000 | tf_op jit(solution)/shard_map/pallas_call | solution.py:60
  56.2 9.2 %all_to_all.34.in_ref = bf16[8,64,384]{2,1,0:T(8,128)(2,1)S(1)} all-to-all(bf16[8,64,384]{2,1,0:T(8,128)(2,1)S(1)} %shard_map.131), channel_id=1, replica_groups=mesh['zh'=4,'zl'=2,'y'=4,'core'=2,'tp'=4] {'zl','y'}, dimensions={0} | all-to-all | bytes 786432 | tf_op jit(solution)/shard_map/all_to_all | solution.py:396
  65.5 0.1 shard_map.132
  65.5 10.3 %all_to_all.35.in_ref = bf16[4,64,384]{2,1,0:T(8,128)(2,1)S(1)} all-to-all(bf16[4,64,384]{2,1,0:T(8,128)(2,1)S(1)} %shard_map.132), channel_id=1, replica_groups=mesh['zh'=4,'zl'=2,'y'=4,'core'=2,'tp'=4] {'zh'}, dimensions={0} | all-to-all | bytes 393216 | tf_op jit(solution)/shard_map/all_to_all | solution.py:396
  75.9 8.2 %collective-permute-start.3 = (bf16[64,384]{1,0:T(8,128)(2,1)S(1)}, bf16[64,384]{1,0:T(8,128)(2,1)S(1)}, u32[]{:S(2)}, u32[]{:S(2)}) collective-permute-start(bf16[64,384]{1,0:T(8,128)(2,1)S(1)} %shard_map.133.own_ref), channel_id=1, source_target_pairs={{0,4},{4,0},{1,5},{5,1},{2,6},{6,2},{3,7},{7,3},{8,12},{12,8},{9,1... | collective-permute-start | bytes 147464 | tf_op jit(solution)/shard_map/ppermute | solution.py:392
  84.1 0.9 %collective-permute-done.3.other_ref = bf16[64,384]{1,0:T(8,128)(2,1)S(1)} collective-permute-done((bf16[64,384]{1,0:T(8,128)(2,1)S(1)}, bf16[64,384]{1,0:T(8,128)(2,1)S(1)}, u32[]{:S(2)}, u32[]{:S(2)}) %collective-permute-start.3) | collective-permute-done | bytes 49184 | tf_op jit(solution)/shard_map/ppermute | solution.py:392
  84.9 0.7 shard_map.134
  (6 shorter events, 0.0 us)
Async XLA Ops:
  0.0 8.5 %collective-permute-start = (bf16[320,384]{1,0:T(8,128)(2,1)}, bf16[320,384]{1,0:T(8,128)(2,1)S(1)}, u32[]{:S(2)}, u32[]{:S(2)}) collective-permute-start(bf16[320,384]{1,0:T(8,128)(2,1)} %bitcast.18), channel_id=1, source_target_pairs={{0,4},{4,0},{1,5},{5,1},{2,6},{6,2},{3,7},{7,3},{8,12},{12,8},{9,1... | collective-permute-start | bytes 737288 | tf_op jit(solution)/shard_map/ppermute | solution.py:392
  3.2 5.3 %collective-permute-start.1 = (bf16[320,384]{1,0:T(8,128)(2,1)}, bf16[320,384]{1,0:T(8,128)(2,1)S(1)}, u32[]{:S(2)}, u32[]{:S(2)}) collective-permute-start(bf16[320,384]{1,0:T(8,128)(2,1)} %bitcast.20), channel_id=1, source_target_pairs={{0,4},{4,0},{1,5},{5,1},{2,6},{6,2},{3,7},{7,3},{8,12},{12,8},{9,1... | collective-permute-start | bytes 737288 | tf_op jit(solution)/shard_map/ppermute | solution.py:392
  3.2 5.3 %collective-permute-start.2 = (bf16[320,384]{1,0:T(8,128)(2,1)}, bf16[320,384]{1,0:T(8,128)(2,1)S(1)}, u32[]{:S(2)}, u32[]{:S(2)}) collective-permute-start(bf16[320,384]{1,0:T(8,128)(2,1)} %bitcast.16), channel_id=1, source_target_pairs={{0,4},{4,0},{1,5},{5,1},{2,6},{6,2},{3,7},{7,3},{8,12},{12,8},{9,1... | collective-permute-start | bytes 737288 | tf_op jit(solution)/shard_map/ppermute | solution.py:392
  3.8 41.0 %copy-start = (bf16[128,1536]{1,0:T(8,128)(2,1)S(1)}, bf16[128,1536]{1,0:T(8,128)(2,1)}, u32[]{:S(2)}) copy-start(bf16[128,1536]{1,0:T(8,128)(2,1)} %tok_ref.1) | copy-start | bytes 1179652
  3.8 41.0 %copy-start.1 = (bf16[1536,384]{1,0:T(8,128)(2,1)S(1)}, bf16[1536,384]{1,0:T(8,128)(2,1)}, u32[]{:S(2)}) copy-start(bf16[1536,384]{1,0:T(8,128)(2,1)} %w_ref.1) | copy-start | bytes 3538948
  3.8 41.0 %copy-start.2 = (bf16[384,40]{0,1:T(8,128)(2,1)S(1)}, bf16[384,40]{0,1:T(8,128)(2,1)}, u32[]{:S(2)}) copy-start(bf16[384,40]{0,1:T(8,128)(2,1)} %param.18) | copy-start | bytes 92164
  3.8 41.0 %copy-start.3 = (s32[128,8]{0,1:T(8,128)S(1)}, s32[128,8]{0,1:T(8,128)}, u32[]{:S(2)}) copy-start(s32[128,8]{0,1:T(8,128)} %param.25) | copy-start | bytes 12292
  75.9 9.1 %collective-permute-start.3 = (bf16[64,384]{1,0:T(8,128)(2,1)S(1)}, bf16[64,384]{1,0:T(8,128)(2,1)S(1)}, u32[]{:S(2)}, u32[]{:S(2)}) collective-permute-start(bf16[64,384]{1,0:T(8,128)(2,1)S(1)} %shard_map.133.own_ref), channel_id=1, source_target_pairs={{0,4},{4,0},{1,5},{5,1},{2,6},{6,2},{3,7},{7,3},{8,12},{12,8},{9,1... | collective-permute-start | bytes 147464 | tf_op jit(solution)/shard_map/ppermute | solution.py:392

commit v7 on v6

--- a/solution.py
+++ b/solution.py
@@ -173,8 +173,9 @@
         s = jnp.where(ok[None], s, FLOOR_SCORE)
         sn = jnp.where(ok_new[None], sn, FLOOR_SCORE)
         m = jnp.maximum(jnp.max(s, axis=-1, keepdims=True), jnp.max(sn, axis=-1, keepdims=True))
-        p = jnp.where(ok[None], jnp.exp(s - m), 0.0)
-        pn = jnp.where(ok_new[None], jnp.exp(sn - m), 0.0)
+        m = jnp.maximum(m, 0.1 * FLOOR_SCORE)
+        p = jnp.exp(s - m)
+        pn = jnp.exp(sn - m)
         mass = jnp.sum(p, axis=-1, keepdims=True) + jnp.sum(pn, axis=-1, keepdims=True)
         acc = dot(p.reshape(192, 256).astype(BF16), v_ref[grp * 256 : grp * 256 + 256, :]) + dot(
             pn.reshape(192, 32).astype(BF16), value_new
@@ -366,18 +367,18 @@
         if down_ref is down0_ref:
             copies[0].wait()
         part = part + dot(spread, down_ref[...])
+    for i in range(4):
+        out_ref[i] = part.astype(BF16)
+
+
+def group_body(in_ref, out_ref):
+    v = sum(in_ref[i].astype(F32) for i in range(4)).astype(BF16)
     for i in range(8):
-        out_ref[i] = part.astype(BF16)
-
-
-def group_body(in_ref, out_ref):
-    v = sum(in_ref[i].astype(F32) for i in range(8)).astype(BF16)
-    for i in range(4):
         out_ref[i] = v
 
 
 def finish_body(in_ref, res_ref, out_ref):
-    out_ref[...] = (res_ref[...] + sum(in_ref[i].astype(F32) for i in range(4))).astype(BF16)
+    out_ref[...] = (res_ref[...] + sum(in_ref[i].astype(F32) for i in range(8))).astype(BF16)
 
 
 def assemble_body(own_ref, other_ref, out_ref):
@@ -462,13 +463,13 @@
     )
     (part,) = call(
         expert_body,
-        [((8, HALF, FEAT), BF16)],
+        [((4, HALF, FEAT), BF16)] ,
         (exchange(picked, "tp"), routes.T, down_there, down),
         raw=(3,),
         scratch=[pltpu.VMEM((units, FEAT), BF16), pltpu.SemaphoreType.DMA((1,))],
     )
-    (part,) = call(group_body, [((4, HALF, FEAT), BF16)], (exchange(part, ("zl", "y")),))
-    (own,) = call(finish_body, [((HALF, FEAT), BF16)], (exchange(part, "zh"), residual))
+    (part,) = call(group_body, [((8, HALF, FEAT), BF16)], (exchange(part, "zh"),))
+    (own,) = call(finish_body, [((HALF, FEAT), BF16)], (exchange(part, ("zl", "y")), residual))
     (out,) = call(assemble_body, [((TOKENS, FEAT), BF16)], (own, swap(own)), pinned=False)
     return out
 

time: 86 us -> 85.8 us (level)
  transfers between devices with their start and end apart: 4 -> 4, of which waited for: 1 -> 1; matrix products, arithmetic and copies ran while one was open for 0% -> 0% of each run, Pallas kernels for 6% -> 5%
where the time goes in v7:
time: 85.8 us; the launch traced here: 85.4 us
  blocking collectives  62.5 us (73%)
  starting transfers between devices  11.8 us (14%)
  Pallas kernels  10.1 us (12%)
  waiting for transfers between devices  0.89 us (1%)
    all_to_all x6, blocking collectives, exchange(): return lax.all_to_all(v, axes, 0, 0, tiled=True)  62.5 us
    ppermute x4, starting transfers between devices, swap(): return lax.ppermute(v, 'core', [(0, 1), (1, 0)])  11.8 us
    pallas_call x8, Pallas kernels, call(): run(*[pltpu.with_memory_space_constraint(a, space[k]) for a, k in zip(arg...  10.1 us
  transfers between devices with their start and end apart: 4, of which 1 were waited for; matrix products, arithmetic and copies ran while one was open for 0% of the time, Pallas kernels for 5%

profile of v7, /device:TPU:1, one launch (start us, length us, event | category | flops | bytes accessed | tf_op | source)
XLA Modules:
  0.0 85.4 jit_solution(13277501758260909713)
XLA Ops:
  0.0 3.2 %collective-permute-start = (bf16[320,384]{1,0:T(8,128)(2,1)}, bf16[320,384]{1,0:T(8,128)(2,1)S(1)}, u32[]{:S(2)}, u32[]{:S(2)}) collective-permute-start(bf16[320,384]{1,0:T(8,128)(2,1)} %bitcast.18), channel_id=1, source_target_pairs={{0,4},{4,0},{1,5},{5,1},{2,6},{6,2},{3,7},{7,3},{8,12},{12,8},{9,1... | collective-permute-start | bytes 737288 | tf_op jit(solution)/shard_map/ppermute | solution.py:393
  3.2 0.0 collective-permute-start.1
  3.2 0.5 collective-permute-start.2
  3.8 4.7 %shard_map.127 = bf16[8,16,512]{2,1,0:T(8,128)(2,1)S(1)} custom-call(s32[32]{0:T(128)} %len_ref.1, bf16[128,1536]{1,0:T(8,128)(2,1)} %tok_ref.1, f32[1536]{0:T(1024)} %gain_hbm.2, bf16[1536,640]{1,0:T(8,128)(2,1)} %w_hbm.1, bf16[1024,128]{1,0:T(8,128)(2,1)} %bitcast.14, bf16[1024,128]{1,0:T(8,128)(2,1)} %bitcast.15), custom_call_target="tpu_custom_call" | custom-call | flops 10000000 | bytes 1000000 | tf_op jit(solution)/shard_map/pallas_call | solution.py:60
  8.5 0.0 collective-permute-done.gate1_ref
  8.5 0.0 collective-permute-done.1.up1_ref
  8.5 0.0 collective-permute-done.2.down1_ref
  8.5 7.9 %all_to_all.30.in_ref = bf16[8,16,512]{2,1,0:T(8,128)(2,1)S(1)} all-to-all(bf16[8,16,512]{2,1,0:T(8,128)(2,1)S(1)} %shard_map.127), channel_id=1, replica_groups=mesh['zh'=4,'zl'=2,'y'=4,'core'=2,'tp'=4] {'y','core'}, dimensions={0} | all-to-all | bytes 262144 | tf_op jit(solution)/shard_map/all_to_all | solution.py:397
  16.4 0.4 shard_map.128
  16.8 15.8 %all_to_all.31.in_ref = bf16[8,16,512]{2,1,0:T(8,128)(2,1)S(1)} all-to-all(bf16[8,16,512]{2,1,0:T(8,128)(2,1)S(1)} %shard_map.128), channel_id=1, replica_groups=mesh['zh'=4,'zl'=2,'y'=4,'core'=2,'tp'=4] {'zh','zl'}, dimensions={0} | all-to-all | bytes 262144 | tf_op jit(solution)/shard_map/all_to_all | solution.py:397
  32.6 0.4 shard_map.129
  33.0 11.7 %all_to_all.32.mine_ref = bf16[16,16,384]{2,1,0:T(8,128)(2,1)S(1)} all-to-all(bf16[16,16,384]{2,1,0:T(8,128)(2,1)S(1)} %shard_map.129), channel_id=1, replica_groups=mesh['zh'=4,'zl'=2,'y'=4,'core'=2,'tp'=4] {'y','tp'}, dimensions={0} | all-to-all | bytes 393216 | tf_op jit(solution)/shard_map/all_to_all | solution.py:397
  44.7 0.0 copy-done
  44.7 0.0 copy-done.1
  44.7 0.0 copy-done.2
  44.7 2.7 %shard_map.130 = (f32[64,384]{1,0:T(8,128)S(1)}, bf16[4,64,384]{2,1,0:T(8,128)(2,1)S(1)}) custom-call(bf16[16,16,384]{2,1,0:T(8,128)(2,1)S(1)} %all_to_all.32.mine_ref, bf16[1536,384]{1,0:T(8,128)(2,1)S(1)} %copy-done.1, bf16[128,1536]{1,0:T(8,128)(2,1)S(1)} %copy-done, bf16[40,384]{1,0:T(8,128)(2,1)S(1)} %bitcast.11, s32[8,128]{1,0:T(8,128)S(1)} %bitcast.12, ...), custom_call_target="tpu_custom_call" | custom-call | flops 10000000 | bytes 1000000 | tf_op jit(solution)/shard_map/pallas_call | solution.py:60
  47.5 7.5 %all_to_all.33.in_ref = bf16[4,64,384]{2,1,0:T(8,128)(2,1)S(1)} all-to-all(bf16[4,64,384]{2,1,0:T(8,128)(2,1)S(1)} %get-tuple-element.14), channel_id=1, replica_groups=mesh['zh'=4,'zl'=2,'y'=4,'core'=2,'tp'=4] {'tp'}, dimensions={0} | all-to-all | bytes 393216 | tf_op jit(solution)/shard_map/all_to_all | solution.py:397
  55.0 1.2 %shard_map.131 = bf16[4,64,384]{2,1,0:T(8,128)(2,1)S(1)} custom-call(bf16[4,64,384]{2,1,0:T(8,128)(2,1)S(1)} %all_to_all.33.in_ref, s32[8,128]{1,0:T(8,128)S(1)} %bitcast.13, bf16[320,384]{1,0:T(8,128)(2,1)S(1)} %collective-permute-done.2.down1_ref, bf16[320,384]{1,0:T(8,128)(2,1)} %bitcast.17), custom_call_target="tpu_custom_call" | custom-call | flops 10000000 | bytes 1000000 | tf_op jit(solution)/shard_map/pallas_call | solution.py:60
  56.2 10.3 %all_to_all.34.in_ref = bf16[4,64,384]{2,1,0:T(8,128)(2,1)S(1)} all-to-all(bf16[4,64,384]{2,1,0:T(8,128)(2,1)S(1)} %shard_map.131), channel_id=1, replica_groups=mesh['zh'=4,'zl'=2,'y'=4,'core'=2,'tp'=4] {'zh'}, dimensions={0} | all-to-all | bytes 393216 | tf_op jit(solution)/shard_map/all_to_all | solution.py:397
  66.5 9.2 %all_to_all.35.in_ref = bf16[8,64,384]{2,1,0:T(8,128)(2,1)S(1)} all-to-all(bf16[8,64,384]{2,1,0:T(8,128)(2,1)S(1)} %shard_map.132), channel_id=1, replica_groups=mesh['zh'=4,'zl'=2,'y'=4,'core'=2,'tp'=4] {'zl','y'}, dimensions={0} | all-to-all | bytes 786432 | tf_op jit(solution)/shard_map/all_to_all | solution.py:397
  75.8 0.1 shard_map.133.own_ref
  75.8 8.0 %collective-permute-start.3 = (bf16[64,384]{1,0:T(8,128)(2,1)S(1)}, bf16[64,384]{1,0:T(8,128)(2,1)S(1)}, u32[]{:S(2)}, u32[]{:S(2)}) collective-permute-start(bf16[64,384]{1,0:T(8,128)(2,1)S(1)} %shard_map.133.own_ref), channel_id=1, source_target_pairs={{0,4},{4,0},{1,5},{5,1},{2,6},{6,2},{3,7},{7,3},{8,12},{12,8},{9,1... | collective-permute-start | bytes 147464 | tf_op jit(solution)/shard_map/ppermute | solution.py:393
  83.9 0.9 %collective-permute-done.3.other_ref = bf16[64,384]{1,0:T(8,128)(2,1)S(1)} collective-permute-done((bf16[64,384]{1,0:T(8,128)(2,1)S(1)}, bf16[64,384]{1,0:T(8,128)(2,1)S(1)}, u32[]{:S(2)}, u32[]{:S(2)}) %collective-permute-start.3) | collective-permute-done | bytes 49184 | tf_op jit(solution)/shard_map/ppermute | solution.py:393
  84.7 0.7 shard_map.134
  (6 shorter events, 0.0 us)
Async XLA Ops:
  0.0 8.5 %collective-permute-start = (bf16[320,384]{1,0:T(8,128)(2,1)}, bf16[320,384]{1,0:T(8,128)(2,1)S(1)}, u32[]{:S(2)}, u32[]{:S(2)}) collective-permute-start(bf16[320,384]{1,0:T(8,128)(2,1)} %bitcast.18), channel_id=1, source_target_pairs={{0,4},{4,0},{1,5},{5,1},{2,6},{6,2},{3,7},{7,3},{8,12},{12,8},{9,1... | collective-permute-start | bytes 737288 | tf_op jit(solution)/shard_map/ppermute | solution.py:393
  3.2 5.2 %collective-permute-start.1 = (bf16[320,384]{1,0:T(8,128)(2,1)}, bf16[320,384]{1,0:T(8,128)(2,1)S(1)}, u32[]{:S(2)}, u32[]{:S(2)}) collective-permute-start(bf16[320,384]{1,0:T(8,128)(2,1)} %bitcast.20), channel_id=1, source_target_pairs={{0,4},{4,0},{1,5},{5,1},{2,6},{6,2},{3,7},{7,3},{8,12},{12,8},{9,1... | collective-permute-start | bytes 737288 | tf_op jit(solution)/shard_map/ppermute | solution.py:393
  3.2 5.2 %collective-permute-start.2 = (bf16[320,384]{1,0:T(8,128)(2,1)}, bf16[320,384]{1,0:T(8,128)(2,1)S(1)}, u32[]{:S(2)}, u32[]{:S(2)}) collective-permute-start(bf16[320,384]{1,0:T(8,128)(2,1)} %bitcast.16), channel_id=1, source_target_pairs={{0,4},{4,0},{1,5},{5,1},{2,6},{6,2},{3,7},{7,3},{8,12},{12,8},{9,1... | collective-permute-start | bytes 737288 | tf_op jit(solution)/shard_map/ppermute | solution.py:393
  3.8 41.0 %copy-start = (bf16[128,1536]{1,0:T(8,128)(2,1)S(1)}, bf16[128,1536]{1,0:T(8,128)(2,1)}, u32[]{:S(2)}) copy-start(bf16[128,1536]{1,0:T(8,128)(2,1)} %tok_ref.1) | copy-start | bytes 1179652
  3.8 41.0 %copy-start.1 = (bf16[1536,384]{1,0:T(8,128)(2,1)S(1)}, bf16[1536,384]{1,0:T(8,128)(2,1)}, u32[]{:S(2)}) copy-start(bf16[1536,384]{1,0:T(8,128)(2,1)} %w_ref.1) | copy-start | bytes 3538948
  3.8 41.0 %copy-start.2 = (bf16[384,40]{0,1:T(8,128)(2,1)S(1)}, bf16[384,40]{0,1:T(8,128)(2,1)}, u32[]{:S(2)}) copy-start(bf16[384,40]{0,1:T(8,128)(2,1)} %param.18) | copy-start | bytes 92164
  3.8 41.0 %copy-start.3 = (s32[128,8]{0,1:T(8,128)S(1)}, s32[128,8]{0,1:T(8,128)}, u32[]{:S(2)}) copy-start(s32[128,8]{0,1:T(8,128)} %param.25) | copy-start | bytes 12292
  75.8 8.9 %collective-permute-start.3 = (bf16[64,384]{1,0:T(8,128)(2,1)S(1)}, bf16[64,384]{1,0:T(8,128)(2,1)S(1)}, u32[]{:S(2)}, u32[]{:S(2)}) collective-permute-start(bf16[64,384]{1,0:T(8,128)(2,1)S(1)} %shard_map.133.own_ref), channel_id=1, source_target_pairs={{0,4},{4,0},{1,5},{5,1},{2,6},{6,2},{3,7},{7,3},{8,12},{12,8},{9,1... | collective-permute-start | bytes 147464 | tf_op jit(solution)/shard_map/ppermute | solution.py:393
